TPU v7x, 512 devices: a whole 4x8x8 slice. The times are simulated.
512 devices in a mesh: aux: 32 (over x_lo, y, core), pair: 16 (over z, x_hi).
Axes of the slice: x: 4 (x_hi: 2, x_lo: 2; x = x_hi * 2 + x_lo), y: 8, z: 8, core: 2. Of those that a mesh axis runs over, the one named last changes fastest.
Arguments:
- integrals: bfloat16 [4096, 32, 512], P('aux', 'pair'), may hold values from -0.5 to 0.5
- occ_density: bfloat16 [32, 32], replicated, may hold values from -1 to 1
- virt_density: bfloat16 [512, 512], replicated, may hold values from -0.25 to 0.25
- screen: int32 [64, 32], P('aux', 'pair'), may hold values 0 or 1
Outputs:
- polar: float32 [4096, 4096], P('aux', 'pair')
All inputs are finite; a program needn't handle non-finite values. No bound on the sum of `screen` on one device may be relied on, other than what follows from the above.
Results may differ from a plain program's by a relative error of at most 0.0041.
Values may be sent and summed in bfloat16 or wider, within the bound.
No kernel may reach another device: no remote copies, remote signals or barrier semaphores. Data moves between devices by JAX's collectives and lax.ppermute only.
A program may use at most 64 MiB of HBM per device.

v0:
```python
import jax
import jax.numpy as jnp
from jax import lax
from jax.experimental import pallas as pl
from jax.experimental.pallas import tpu as pltpu
from jax.sharding import Mesh, PartitionSpec as P


AUX = ("x_lo", "y", "core")
PAIR = ("z", "x_hi")
PLANE = ("x_lo", "core", "z", "x_hi")
WIDE = ("x_lo", "core", "x_hi")


def ring(step):
    return [(y, (y + step) % 8) for y in range(8)]


def wide_index(place, core):
    return place % 2 * 4 + core * 2 + place // 2


def x_hop(first):
    pairs = []
    for place in range(4):
        for core in range(2):
            step = 1 if (core == 0) == first else -1
            pairs.append((wide_index(place, core), wide_index((place + step) % 4, core)))
    return pairs


def pack(values):
    pieces = values.reshape(2, 2, 2, 16, 2, 8, 64)
    return pieces.transpose(0, 1, 5, 2, 3, 4, 6).reshape(64, 16, 128)


def unpack(got):
    return got.reshape(4, 16, 16, 128).transpose(0, 2, 1, 3).reshape(64, 2048)


def multiply_kernel(where_ref, *refs):
    columns, mine, other, (out_ref, left, right, done) = refs[:9], refs[9:13], refs[13], refs[14:]
    y, place, core = where_ref[0], where_ref[1], where_ref[2]
    copies = []

    def bring(source, target):
        copies.append(pltpu.make_async_copy(source, target, done.at[len(copies)]))
        copies[-1].start()

    for i, steps in enumerate((0, 1, 2, 3, -1, -2, -3)):
        at = lax.rem(y - steps + 8, 8)
        bring(columns[i], left.at[pl.ds(pl.multiple_of(at * 64, 64), 64), :])
    at = lax.rem(y + 4, 8)
    bring(columns[7], left.at[pl.ds(pl.multiple_of(at * 64, 32), 32), :])
    bring(columns[8], left.at[pl.ds(pl.multiple_of(at * 64 + 32, 32), 32), :])
    sign = 1 - 2 * core
    for i, steps in enumerate((0, 1, 2, -1)):
        for near in range(2):
            step = sign * steps if near else -sign * steps
            source = lax.rem(place - step + 8, 4)
            owner = core if near else 1 - core
            at = lax.rem(source, 2) * 4 + owner * 2 + source // 2
            bring(mine[i] if near else other.at[i], right.at[:, pl.ds(pl.multiple_of(at * 16, 16), 16), :])
    for copy in copies:
        copy.wait()
    for part_id in range(2):
        part = lax.dot_general(
            left[part_id * 256 : part_id * 256 + 256, :],
            right[...].reshape(512, 2048),
            (((1,), (1,)), ((), ())),
            preferred_element_type=jnp.float32,
        ).astype(jnp.bfloat16)
        for y_column in range(4):
            for x_lo_q in range(2):
                for group in range(4):
                    row = y_column * 64 + x_lo_q * 32
                    dest = group * 16 + (x_lo_q * 4 + part_id * 2 + y_column // 2) * 2 + y_column % 2
                    out_ref[dest] = part[row : row + 32, group * 128 : group * 128 + 128]


def multiply(where, columns, mine, other):
    mine = [block.reshape(4, 16, 2048) for block in mine]
    return pl.pallas_call(
        multiply_kernel,
        out_shape=jax.ShapeDtypeStruct((64, 32, 128), jnp.bfloat16),
        in_specs=[pl.BlockSpec(memory_space=pltpu.SMEM)] + [pl.BlockSpec(memory_space=pl.ANY)] * 14,
        out_specs=pl.BlockSpec(memory_space=pltpu.VMEM),
        scratch_shapes=[
            pltpu.VMEM((512, 2048), jnp.bfloat16),
            pltpu.VMEM((4, 128, 2048), jnp.bfloat16),
            pltpu.SemaphoreType.DMA((17,)),
        ],
        compiler_params=pltpu.CompilerParams(vmem_limit_bytes=16 * 1024 * 1024),
        cost_estimate=pl.CostEstimate(flops=2 * 512 * 512 * 2048, bytes_accessed=4 << 20, transcendentals=0),
    )(where, *columns, *mine, other.reshape(4, 4, 16, 2048))


def body(integrals, occ_density, virt_density, screen):
    aux_rows, local_pairs, orbitals = integrals.shape
    blocks = screen.shape[0]
    grouped = integrals.reshape(blocks, aux_rows // blocks, local_pairs, orbitals)
    screened = jnp.where(screen[:, None, :, None] > 0, grouped, jnp.zeros_like(grouped)).reshape(
        aux_rows, local_pairs, orbitals
    )
    virtual = jnp.dot(
        screened.reshape(aux_rows * local_pairs, orbitals),
        virt_density,
        preferred_element_type=jnp.float32,
    ).astype(jnp.bfloat16).reshape(aux_rows, local_pairs, orbitals)
    both = jnp.concatenate([pack(screened), pack(virtual)], axis=1)
    got = lax.all_to_all(both, PLANE, 0, 0, tiled=True)
    own = unpack(got[:, :16])
    up1 = lax.ppermute(own, "y", ring(1))
    down1 = lax.ppermute(own, "y", ring(-1))
    up2 = lax.ppermute(up1, "y", ring(1))
    down2 = lax.ppermute(down1, "y", ring(-1))
    up3 = lax.ppermute(up2, "y", ring(1))
    down3 = lax.ppermute(down2, "y", ring(-1))
    up4 = lax.ppermute(up3[:32], "y", ring(1))
    down4 = lax.ppermute(down3[32:], "y", ring(-1))
    columns = [own, up1, up2, up3, down1, down2, down3, up4, down4]
    virt_rows = unpack(got[:, 16:]).reshape(64, 32, 64)
    occupied = jnp.einsum("pms,ml->pls", virt_rows, occ_density, preferred_element_type=jnp.float32)
    occupied = occupied.astype(jnp.bfloat16).reshape(64, 2048)
    near = lax.ppermute(occupied, WIDE, x_hop(True))
    back = lax.ppermute(occupied, WIDE, x_hop(False))
    far = lax.ppermute(near, WIDE, x_hop(True))
    mine = [occupied, near, far, back]
    other = lax.ppermute(jnp.stack(mine), "core", [(0, 1), (1, 0)])
    place = lax.axis_index("x_hi") * 2 + lax.axis_index("x_lo")
    where = jnp.stack([lax.axis_index("y"), place, lax.axis_index("core")]).astype(jnp.int32)
    tiles = multiply(where, columns, mine, other)
    got = lax.all_to_all(tiles, PLANE, 0, 0, tiled=True)
    total = jnp.sum(got.reshape(2, 2, 8, 2, 2, 16, 128).astype(jnp.float32), axis=2)
    return total.transpose(5, 3, 0, 1, 2, 4).reshape(128, 256)


def solution(mesh):
    fine = Mesh(mesh.devices.reshape(2, 8, 2, 8, 2), AUX + PAIR)
    placed = (P(AUX, PAIR, None), P(), P(), P(AUX, PAIR))

    return jax.shard_map(body, mesh=fine, in_specs=placed, out_specs=P(AUX, PAIR), check_vma=False)
```

profile of v0, /device:TPU:30, one launch (start us, length us, event | category | flops | bytes accessed | tf_op | source)
XLA Modules:
  0.0 139.8 jit_solution(15243501600624544709)
XLA Ops:
  0.0 1.1 reshape.48
  1.2 0.3 reshape.46
  1.5 0.3 copy-done.12
  1.8 0.1 broadcast_in_dim.23
  2.0 0.3 convolution_convert_fusion.1
  2.4 0.3 reshape_reshape.11
  2.6 0.5 copy.25
  3.2 0.2 reshape.49
  3.4 0.6 fusion.1
  4.0 0.2 reshape.47
  4.3 32.2 %all_to_all.10 = bf16[64,32,128]{2,1,0:T(8,128)(2,1)S(1)} all-to-all(bf16[64,32,128]{2,1,0:T(8,128)(2,1)S(1)} %pad_maximum_fusion.1), channel_id=1, replica_groups=mesh['x_lo'=2,'y'=8,'core'=2,'z'=8,'x_hi'=2] {'x_lo','core','z','x_hi'}, dimensions={0} | all-to-all | bytes 1048576 | tf_op jit(solution)/shard_map/all_to_all | solution.py:111
  36.6 0.2 reshape_reshape.12
  36.9 0.4 copy-done.11
  37.3 0.3 fusion
  37.6 0.5 reshape.53
  38.1 2.2 %collective-permute-start.8 = (bf16[64,2048]{1,0:T(8,128)(2,1)S(1)}, bf16[64,2048]{1,0:T(8,128)(2,1)S(1)}, u32[]{:S(2)}, u32[]{:S(2)}) collective-permute-start(bf16[64,2048]{1,0:T(8,128)(2,1)S(1)} %reshape.53), channel_id=1, source_target_pairs={{0,256},{16,273},{256,1},{272,16},{1,257},{17,272},{257,0},{273,17... | collective-permute-start | bytes 786440 | tf_op jit(solution)/shard_map/ppermute | solution.py:125
  40.3 3.6 %collective-permute-start.10 = (bf16[64,2048]{1,0:T(8,128)(2,1)S(1)}, bf16[64,2048]{1,0:T(8,128)(2,1)S(1)}, u32[]{:S(2)}, u32[]{:S(2)}) collective-permute-start(bf16[64,2048]{1,0:T(8,128)(2,1)S(1)} %reshape.53), channel_id=1, source_target_pairs={{0,257},{16,272},{256,0},{272,17},{1,256},{17,273},{257,1},{273,16... | collective-permute-start | bytes 786440 | tf_op jit(solution)/shard_map/ppermute | solution.py:126
  44.0 5.2 %collective-permute-done.8 = bf16[64,2048]{1,0:T(8,128)(2,1)S(1)} collective-permute-done((bf16[64,2048]{1,0:T(8,128)(2,1)S(1)}, bf16[64,2048]{1,0:T(8,128)(2,1)S(1)}, u32[]{:S(2)}, u32[]{:S(2)}) %collective-permute-start.8) | collective-permute-done | bytes 262176 | tf_op jit(solution)/shard_map/ppermute | solution.py:125
  49.2 1.9 %collective-permute-start.9 = (bf16[64,2048]{1,0:T(8,128)(2,1)S(1)}, bf16[64,2048]{1,0:T(8,128)(2,1)S(1)}, u32[]{:S(2)}, u32[]{:S(2)}) collective-permute-start(bf16[64,2048]{1,0:T(8,128)(2,1)S(1)} %collective-permute-done.8), channel_id=1, source_target_pairs={{0,256},{16,273},{256,1},{272,16},{1,257},{17,272},{257,0},{273,17... | collective-permute-start | bytes 786440 | tf_op jit(solution)/shard_map/ppermute | solution.py:127
  51.1 0.5 stack_reshape.3
  51.5 5.9 %collective-permute-done.9 = bf16[64,2048]{1,0:T(8,128)(2,1)S(1)} collective-permute-done((bf16[64,2048]{1,0:T(8,128)(2,1)S(1)}, bf16[64,2048]{1,0:T(8,128)(2,1)S(1)}, u32[]{:S(2)}, u32[]{:S(2)}) %collective-permute-start.9) | collective-permute-done | bytes 262176 | tf_op jit(solution)/shard_map/ppermute | solution.py:127
  57.4 1.1 pad_maximum_fusion
  58.5 1.9 %collective-permute-start.11 = (bf16[4,64,2048]{2,1,0:T(8,128)(2,1)}, bf16[4,64,2048]{2,1,0:T(8,128)(2,1)S(1)}, u32[]{:S(2)}, u32[]{:S(2)}) collective-permute-start(bf16[4,64,2048]{2,1,0:T(8,128)(2,1)} %pad_maximum_fusion), channel_id=1, source_target_pairs={{0,16},{16,0},{1,17},{17,1},{2,18},{18,2},{3,19},{19,3},{4,20},{20... | collective-permute-start | bytes 3145736 | tf_op jit(solution)/shard_map/ppermute | solution.py:129
  60.6 4.7 %collective-permute-start = (bf16[64,2048]{1,0:T(8,128)(2,1)S(1)}, bf16[64,2048]{1,0:T(8,128)(2,1)S(1)}, u32[]{:S(2)}, u32[]{:S(2)}) collective-permute-start(bf16[64,2048]{1,0:T(8,128)(2,1)S(1)} %bitcast.40), channel_id=1, source_target_pairs={{0,32},{32,64},{64,96},{96,128},{128,160},{160,192},{192,224},{224... | collective-permute-start | bytes 786440 | tf_op jit(solution)/shard_map/ppermute | solution.py:113
  65.3 1.9 %collective-permute-start.3 = (bf16[64,2048]{1,0:T(8,128)(2,1)S(1)}, bf16[64,2048]{1,0:T(8,128)(2,1)S(1)}, u32[]{:S(2)}, u32[]{:S(2)}) collective-permute-start(bf16[64,2048]{1,0:T(8,128)(2,1)S(1)} %bitcast.41), channel_id=1, source_target_pairs={{0,224},{32,0},{64,32},{96,64},{128,96},{160,128},{192,160},{224,1... | collective-permute-start | bytes 786440 | tf_op jit(solution)/shard_map/ppermute | solution.py:114
  67.3 4.3 %collective-permute-done.refs_1_ = bf16[64,2048]{1,0:T(8,128)(2,1)S(1)} collective-permute-done((bf16[64,2048]{1,0:T(8,128)(2,1)S(1)}, bf16[64,2048]{1,0:T(8,128)(2,1)S(1)}, u32[]{:S(2)}, u32[]{:S(2)}) %collective-permute-start) | collective-permute-done | bytes 262176 | tf_op jit(solution)/shard_map/ppermute | solution.py:113
  71.5 5.6 %collective-permute-start.1 = (bf16[64,2048]{1,0:T(8,128)(2,1)S(1)}, bf16[64,2048]{1,0:T(8,128)(2,1)S(1)}, u32[]{:S(2)}, u32[]{:S(2)}) collective-permute-start(bf16[64,2048]{1,0:T(8,128)(2,1)S(1)} %collective-permute-done.refs_1_), channel_id=1, source_target_pairs={{0,32},{32,64},{64,96},{96,128},{128,160},{160,192},{192,224},{224... | collective-permute-start | bytes 786440 | tf_op jit(solution)/shard_map/ppermute | solution.py:115
  77.1 1.9 %collective-permute-start.4 = (bf16[64,2048]{1,0:T(8,128)(2,1)S(1)}, bf16[64,2048]{1,0:T(8,128)(2,1)S(1)}, u32[]{:S(2)}, u32[]{:S(2)}) collective-permute-start(bf16[64,2048]{1,0:T(8,128)(2,1)S(1)} %collective-permute-done.3.refs_4_), channel_id=1, source_target_pairs={{0,224},{32,0},{64,32},{96,64},{128,96},{160,128},{192,160},{224,1... | collective-permute-start | bytes 786440 | tf_op jit(solution)/shard_map/ppermute | solution.py:116
  79.1 0.7 copy-done.3
  79.8 2.7 %collective-permute-done.1.refs_2_ = bf16[64,2048]{1,0:T(8,128)(2,1)S(1)} collective-permute-done((bf16[64,2048]{1,0:T(8,128)(2,1)S(1)}, bf16[64,2048]{1,0:T(8,128)(2,1)S(1)}, u32[]{:S(2)}, u32[]{:S(2)}) %collective-permute-start.1) | collective-permute-done | bytes 262176 | tf_op jit(solution)/shard_map/ppermute | solution.py:115
  82.5 5.6 %collective-permute-start.2 = (bf16[64,2048]{1,0:T(8,128)(2,1)S(1)}, bf16[64,2048]{1,0:T(8,128)(2,1)S(1)}, u32[]{:S(2)}, u32[]{:S(2)}) collective-permute-start(bf16[64,2048]{1,0:T(8,128)(2,1)S(1)} %collective-permute-done.1.refs_2_), channel_id=1, source_target_pairs={{0,32},{32,64},{64,96},{96,128},{128,160},{160,192},{192,224},{224... | collective-permute-start | bytes 786440 | tf_op jit(solution)/shard_map/ppermute | solution.py:117
  88.1 0.7 copy-done.5
  88.8 1.9 %collective-permute-start.5 = (bf16[64,2048]{1,0:T(8,128)(2,1)S(1)}, bf16[64,2048]{1,0:T(8,128)(2,1)S(1)}, u32[]{:S(2)}, u32[]{:S(2)}) collective-permute-start(bf16[64,2048]{1,0:T(8,128)(2,1)S(1)} %collective-permute-done.4.refs_5_), channel_id=1, source_target_pairs={{0,224},{32,0},{64,32},{96,64},{128,96},{160,128},{192,160},{224,1... | collective-permute-start | bytes 786440 | tf_op jit(solution)/shard_map/ppermute | solution.py:118
  90.7 1.9 %collective-permute-done.2.refs_3_ = bf16[64,2048]{1,0:T(8,128)(2,1)S(1)} collective-permute-done((bf16[64,2048]{1,0:T(8,128)(2,1)S(1)}, bf16[64,2048]{1,0:T(8,128)(2,1)S(1)}, u32[]{:S(2)}, u32[]{:S(2)}) %collective-permute-start.2) | collective-permute-done | bytes 262176 | tf_op jit(solution)/shard_map/ppermute | solution.py:117
  92.6 0.7 slice.17
  93.2 5.6 %collective-permute-start.6 = (bf16[32,2048]{1,0:T(8,128)(2,1)}, bf16[32,2048]{1,0:T(8,128)(2,1)S(1)}, u32[]{:S(2)}, u32[]{:S(2)}) collective-permute-start(bf16[32,2048]{1,0:T(8,128)(2,1)} %slice.17), channel_id=1, source_target_pairs={{0,32},{32,64},{64,96},{96,128},{128,160},{160,192},{192,224},{224... | collective-permute-start | bytes 393224 | tf_op jit(solution)/shard_map/ppermute | solution.py:119
  98.8 0.7 slice.18
  99.5 1.9 %collective-permute-start.7 = (bf16[32,2048]{1,0:T(8,128)(2,1)}, bf16[32,2048]{1,0:T(8,128)(2,1)}, u32[]{:S(2)}, u32[]{:S(2)}) collective-permute-start(bf16[32,2048]{1,0:T(8,128)(2,1)} %slice.18), channel_id=1, source_target_pairs={{0,224},{32,0},{64,32},{96,64},{128,96},{160,128},{192,160},{224,1... | collective-permute-start | bytes 393224 | tf_op jit(solution)/shard_map/ppermute | solution.py:120
  101.4 0.1 pad_add_fusion.where_ref
  101.5 1.5 %reshape_reshape.13.refs_9_ = bf16[4,16,2048]{2,1,0:T(8,128)(2,1)S(1)} reshape(bf16[64,32,64]{2,1,0:T(8,128)(2,1)} %copy-done.9) | data formatting | bytes 524288 | tf_op jit(solution)/shard_map/reshape;reshape | solution.py:82
  103.0 4.9 %collective-permute-done.7.refs_8_ = bf16[32,2048]{1,0:T(8,128)(2,1)} collective-permute-done((bf16[32,2048]{1,0:T(8,128)(2,1)}, bf16[32,2048]{1,0:T(8,128)(2,1)}, u32[]{:S(2)}, u32[]{:S(2)}) %collective-permute-start.7) | collective-permute-done | bytes 131104 | tf_op jit(solution)/shard_map/ppermute | solution.py:120
  107.9 0.9 copy-done.2
  108.8 0.9 copy-done.4
  109.8 0.9 copy-done.6
  110.7 0.9 copy-done.8
  111.7 3.2 %shard_map.46 = bf16[64,32,128]{2,1,0:T(8,128)(2,1)S(1)} custom-call(s32[3]{0:T(128)S(1)} %pad_add_fusion.where_ref, bf16[64,2048]{1,0:T(8,128)(2,1)S(1)} %bitcast.42, bf16[64,2048]{1,0:T(8,128)(2,1)S(1)} %copy-done.2, bf16[64,2048]{1,0:T(8,128)(2,1)S(1)} %copy-done.6, bf16[64,2048]{1,0:T(8,128)(2,1)S(1)} %collective-permute-done.2.refs_3_, ...), custom_call_target="tpu_custom_call" | custom-call | flops 1073741824 | bytes 4194304 | tf_op jit(solution)/shard_map/pallas_call | solution.py:83
  114.9 24.1 %all_to_all.11 = bf16[64,32,128]{2,1,0:T(8,128)(2,1)S(1)} all-to-all(bf16[64,32,128]{2,1,0:T(8,128)(2,1)S(1)} %shard_map.46), channel_id=1, replica_groups=mesh['x_lo'=2,'y'=8,'core'=2,'z'=8,'x_hi'=2] {'x_lo','core','z','x_hi'}, dimensions={0} | all-to-all | bytes 1048576 | tf_op jit(solution)/shard_map/all_to_all | solution.py:133
  139.1 0.8 copy.18
  (33 shorter events, 0.4 us)
Async XLA Ops:
  0.0 2.0 %copy-start = (bf16[512,512]{1,0:T(8,128)(2,1)S(1)}, bf16[512,512]{1,0:T(8,128)(2,1)}, u32[]{:S(2)}) copy-start(bf16[512,512]{1,0:T(8,128)(2,1)} %param.6) | copy-start | bytes 1572868
  0.0 1.1 copy-start.10
  1.1 0.7 copy-start.12
  36.6 0.7 copy-start.11
  37.6 13.9 %copy-start.9 = (bf16[64,32,64]{2,1,0:T(8,128)(2,1)}, bf16[64,32,64]{2,1,0:T(8,128)(2,1)S(1)}, u32[]{:S(2)}) copy-start(bf16[64,32,64]{2,1,0:T(8,128)(2,1)S(1)} %fusion) | copy-start | bytes 786436
  38.1 11.1 %collective-permute-start.8 = (bf16[64,2048]{1,0:T(8,128)(2,1)S(1)}, bf16[64,2048]{1,0:T(8,128)(2,1)S(1)}, u32[]{:S(2)}, u32[]{:S(2)}) collective-permute-start(bf16[64,2048]{1,0:T(8,128)(2,1)S(1)} %reshape.53), channel_id=1, source_target_pairs={{0,256},{16,273},{256,1},{272,16},{1,257},{17,272},{257,0},{273,17... | collective-permute-start | bytes 786440 | tf_op jit(solution)/shard_map/ppermute | solution.py:125
  40.3 11.2 %collective-permute-start.10 = (bf16[64,2048]{1,0:T(8,128)(2,1)S(1)}, bf16[64,2048]{1,0:T(8,128)(2,1)S(1)}, u32[]{:S(2)}, u32[]{:S(2)}) collective-permute-start(bf16[64,2048]{1,0:T(8,128)(2,1)S(1)} %reshape.53), channel_id=1, source_target_pairs={{0,257},{16,272},{256,0},{272,17},{1,256},{17,273},{257,1},{273,16... | collective-permute-start | bytes 786440 | tf_op jit(solution)/shard_map/ppermute | solution.py:126
  49.2 8.3 %collective-permute-start.9 = (bf16[64,2048]{1,0:T(8,128)(2,1)S(1)}, bf16[64,2048]{1,0:T(8,128)(2,1)S(1)}, u32[]{:S(2)}, u32[]{:S(2)}) collective-permute-start(bf16[64,2048]{1,0:T(8,128)(2,1)S(1)} %collective-permute-done.8), channel_id=1, source_target_pairs={{0,256},{16,273},{256,1},{272,16},{1,257},{17,272},{257,0},{273,17... | collective-permute-start | bytes 786440 | tf_op jit(solution)/shard_map/ppermute | solution.py:127
  58.5 49.3 %collective-permute-start.11 = (bf16[4,64,2048]{2,1,0:T(8,128)(2,1)}, bf16[4,64,2048]{2,1,0:T(8,128)(2,1)S(1)}, u32[]{:S(2)}, u32[]{:S(2)}) collective-permute-start(bf16[4,64,2048]{2,1,0:T(8,128)(2,1)} %pad_maximum_fusion), channel_id=1, source_target_pairs={{0,16},{16,0},{1,17},{17,1},{2,18},{18,2},{3,19},{19,3},{4,20},{20... | collective-permute-start | bytes 3145736 | tf_op jit(solution)/shard_map/ppermute | solution.py:129
  60.6 10.9 %collective-permute-start = (bf16[64,2048]{1,0:T(8,128)(2,1)S(1)}, bf16[64,2048]{1,0:T(8,128)(2,1)S(1)}, u32[]{:S(2)}, u32[]{:S(2)}) collective-permute-start(bf16[64,2048]{1,0:T(8,128)(2,1)S(1)} %bitcast.40), channel_id=1, source_target_pairs={{0,32},{32,64},{64,96},{96,128},{128,160},{160,192},{192,224},{224... | collective-permute-start | bytes 786440 | tf_op jit(solution)/shard_map/ppermute | solution.py:113
  65.3 11.8 %collective-permute-start.3 = (bf16[64,2048]{1,0:T(8,128)(2,1)S(1)}, bf16[64,2048]{1,0:T(8,128)(2,1)S(1)}, u32[]{:S(2)}, u32[]{:S(2)}) collective-permute-start(bf16[64,2048]{1,0:T(8,128)(2,1)S(1)} %bitcast.41), channel_id=1, source_target_pairs={{0,224},{32,0},{64,32},{96,64},{128,96},{160,128},{192,160},{224,1... | collective-permute-start | bytes 786440 | tf_op jit(solution)/shard_map/ppermute | solution.py:114
  71.5 28.0 %copy-start.1 = (bf16[64,2048]{1,0:T(8,128)(2,1)}, bf16[64,2048]{1,0:T(8,128)(2,1)S(1)}, u32[]{:S(2)}) copy-start(bf16[64,2048]{1,0:T(8,128)(2,1)S(1)} %collective-permute-done.refs_1_) | copy-start | bytes 786436
  71.5 10.9 %collective-permute-start.1 = (bf16[64,2048]{1,0:T(8,128)(2,1)S(1)}, bf16[64,2048]{1,0:T(8,128)(2,1)S(1)}, u32[]{:S(2)}, u32[]{:S(2)}) collective-permute-start(bf16[64,2048]{1,0:T(8,128)(2,1)S(1)} %collective-permute-done.refs_1_), channel_id=1, source_target_pairs={{0,32},{32,64},{64,96},{96,128},{128,160},{160,192},{192,224},{224... | collective-permute-start | bytes 786440 | tf_op jit(solution)/shard_map/ppermute | solution.py:115
  77.1 11.6 %collective-permute-start.4 = (bf16[64,2048]{1,0:T(8,128)(2,1)S(1)}, bf16[64,2048]{1,0:T(8,128)(2,1)S(1)}, u32[]{:S(2)}, u32[]{:S(2)}) collective-permute-start(bf16[64,2048]{1,0:T(8,128)(2,1)S(1)} %collective-permute-done.3.refs_4_), channel_id=1, source_target_pairs={{0,224},{32,0},{64,32},{96,64},{128,96},{160,128},{192,160},{224,1... | collective-permute-start | bytes 786440 | tf_op jit(solution)/shard_map/ppermute | solution.py:116
  79.1 0.7 copy-start.3
  82.5 10.1 %collective-permute-start.2 = (bf16[64,2048]{1,0:T(8,128)(2,1)S(1)}, bf16[64,2048]{1,0:T(8,128)(2,1)S(1)}, u32[]{:S(2)}, u32[]{:S(2)}) collective-permute-start(bf16[64,2048]{1,0:T(8,128)(2,1)S(1)} %collective-permute-done.1.refs_2_), channel_id=1, source_target_pairs={{0,32},{32,64},{64,96},{96,128},{128,160},{160,192},{192,224},{224... | collective-permute-start | bytes 786440 | tf_op jit(solution)/shard_map/ppermute | solution.py:117
  88.1 0.7 copy-start.5
  88.8 10.7 %copy-start.7 = (bf16[64,2048]{1,0:T(8,128)(2,1)}, bf16[64,2048]{1,0:T(8,128)(2,1)S(1)}, u32[]{:S(2)}) copy-start(bf16[64,2048]{1,0:T(8,128)(2,1)S(1)} %collective-permute-done.4.refs_5_) | copy-start | bytes 786436
  88.8 10.1 %collective-permute-start.5 = (bf16[64,2048]{1,0:T(8,128)(2,1)S(1)}, bf16[64,2048]{1,0:T(8,128)(2,1)S(1)}, u32[]{:S(2)}, u32[]{:S(2)}) collective-permute-start(bf16[64,2048]{1,0:T(8,128)(2,1)S(1)} %collective-permute-done.4.refs_5_), channel_id=1, source_target_pairs={{0,224},{32,0},{64,32},{96,64},{128,96},{160,128},{192,160},{224,1... | collective-permute-start | bytes 786440 | tf_op jit(solution)/shard_map/ppermute | solution.py:118
  93.2 9.8 %collective-permute-start.6 = (bf16[32,2048]{1,0:T(8,128)(2,1)}, bf16[32,2048]{1,0:T(8,128)(2,1)S(1)}, u32[]{:S(2)}, u32[]{:S(2)}) collective-permute-start(bf16[32,2048]{1,0:T(8,128)(2,1)} %slice.17), channel_id=1, source_target_pairs={{0,32},{32,64},{64,96},{96,128},{128,160},{160,192},{192,224},{224... | collective-permute-start | bytes 393224 | tf_op jit(solution)/shard_map/ppermute | solution.py:119
  99.5 8.4 %collective-permute-start.7 = (bf16[32,2048]{1,0:T(8,128)(2,1)}, bf16[32,2048]{1,0:T(8,128)(2,1)}, u32[]{:S(2)}, u32[]{:S(2)}) collective-permute-start(bf16[32,2048]{1,0:T(8,128)(2,1)} %slice.18), channel_id=1, source_target_pairs={{0,224},{32,0},{64,32},{96,64},{128,96},{160,128},{192,160},{224,1... | collective-permute-start | bytes 393224 | tf_op jit(solution)/shard_map/ppermute | solution.py:120
  107.9 1.0 copy-start.2
  108.8 0.9 copy-start.4
  109.8 0.9 copy-start.6
  110.7 0.9 copy-start.8
where the time goes:
time: 141 us; the launch traced here: 140 us
  blocking collectives  56.2 us (40%)
  starting transfers between devices  38.8 us (28%)
  waiting for transfers between devices  24.8 us (18%)
  local copies, waits for them, and re-layouts  13.9 us (10%)
  Pallas kernels  3.23 us (2%)
  other arithmetic  1.89 us (1%)
    all_to_all x1, blocking collectives, body(): got = lax.all_to_all(both, PLANE, 0, 0, tiled=True)  32.2 us
    all_to_all x1, blocking collectives, body(): got = lax.all_to_all(tiles, PLANE, 0, 0, tiled=True)  24.1 us
    unnamed x27, local copies, waits for them, and re-layouts  6.04 us
    ppermute x1, waiting for transfers between devices, body(): far = lax.ppermute(near, WIDE, x_hop(True))  5.87 us
    ppermute x1, starting transfers between devices, body(): up2 = lax.ppermute(up1, 'y', ring(1))  5.59 us
    ppermute x1, starting transfers between devices, body(): up3 = lax.ppermute(up2, 'y', ring(1))  5.59 us
    ppermute x1, starting transfers between devices, body(): up4 = lax.ppermute(up3[:32], 'y', ring(1))  5.59 us
    ppermute x1, waiting for transfers between devices, body(): near = lax.ppermute(occupied, WIDE, x_hop(True))  5.21 us
  transfers between devices with their start and end apart: 12, of which 6 were waited for; matrix products, arithmetic and copies ran while one was open for 2% of the time, Pallas kernels for 0%

commit v1 on v0

v1 whole, which is shorter than its diff:
```python
import jax
import jax.numpy as jnp
from jax import lax
from jax.experimental import pallas as pl
from jax.experimental.pallas import tpu as pltpu
from jax.sharding import Mesh, PartitionSpec as P


AUX = ("x_lo", "y_hi", "y_lo", "core")
PAIR = ("z", "x_hi")
GROUP = ("x_lo", "y_lo", "core", "z", "x_hi")
WIDE = ("x_lo", "core", "x_hi")
TALL = ("y_hi", "core")


def ring(step):
    return [(y, (y + step) % 4) for y in range(4)]


def y_hop():
    return [(y * 2 + core, (y + 1 - 2 * core) % 4 * 2 + core) for y in range(4) for core in range(2)]


def wide_index(place, core):
    return place % 2 * 4 + core * 2 + place // 2


def x_hop(first):
    pairs = []
    for place in range(4):
        for core in range(2):
            step = 1 if (core == 0) == first else -1
            pairs.append((wide_index(place, core), wide_index((place + step) % 4, core)))
    return pairs


def pack(both):
    pieces = both.reshape(2, 2, 2, 2, 16, 2, 8, 2, 32)
    return pieces.transpose(1, 7, 2, 6, 3, 4, 0, 5, 8).reshape(128, 16, 128)


def unpack(got):
    return got.reshape(8, 16, 16, 64).transpose(0, 2, 1, 3).reshape(128, 1024)


def multiply_kernel(where_ref, *refs):
    columns, mine, other, (out_ref, left, right, done) = refs[:4], refs[4:8], refs[8], refs[9:]
    y, place, core = where_ref[0], where_ref[1], where_ref[2]
    copies = []

    def bring(source, target):
        copies.append(pltpu.make_async_copy(source, target, done.at[len(copies)]))
        copies[-1].start()

    for i, steps in enumerate((0, 1, -1, 2)):
        at = lax.rem(y - steps + 4, 4)
        bring(columns[i], left.at[pl.ds(pl.multiple_of(at * 128, 128), 128), :])
    sign = 1 - 2 * core
    for i, steps in enumerate((0, 1, 2, -1)):
        for near in range(2):
            step = sign * steps if near else -sign * steps
            source = lax.rem(place - step + 8, 4)
            owner = core if near else 1 - core
            at = lax.rem(source, 2) * 4 + owner * 2 + source // 2
            bring(mine[i] if near else other.at[i], right.at[:, pl.ds(pl.multiple_of(at * 16, 16), 16), :])
    for copy in copies:
        copy.wait()
    for part_id in range(4):
        part = lax.dot_general(
            left[part_id * 128 : part_id * 128 + 128, :],
            right[...].reshape(1024, 1024),
            (((1,), (1,)), ((), ())),
            preferred_element_type=jnp.float32,
        ).astype(jnp.bfloat16)
        for x_lo_q in range(2):
            for y_lo_q in range(2):
                for group in range(8):
                    row = x_lo_q * 64 + y_lo_q * 32
                    dest = group * 16 + (x_lo_q * 4 + part_id) * 2 + y_lo_q
                    out_ref[dest] = part[row : row + 32, group * 128 : group * 128 + 128]


def multiply(where, columns, mine, other):
    mine = [block.reshape(8, 16, 1024) for block in mine]
    return pl.pallas_call(
        multiply_kernel,
        out_shape=jax.ShapeDtypeStruct((128, 32, 128), jnp.bfloat16),
        in_specs=[pl.BlockSpec(memory_space=pltpu.SMEM)] + [pl.BlockSpec(memory_space=pl.ANY)] * 9,
        out_specs=pl.BlockSpec(memory_space=pltpu.VMEM),
        scratch_shapes=[
            pltpu.VMEM((512, 1024), jnp.bfloat16),
            pltpu.VMEM((8, 128, 1024), jnp.bfloat16),
            pltpu.SemaphoreType.DMA((12,)),
        ],
        compiler_params=pltpu.CompilerParams(vmem_limit_bytes=16 * 1024 * 1024),
        cost_estimate=pl.CostEstimate(flops=2 * 512 * 1024 * 1024, bytes_accessed=4 << 20, transcendentals=0),
    )(where, *columns, *mine, other.reshape(4, 8, 16, 1024))


def body(integrals, occ_density, virt_density, screen):
    aux_rows, local_pairs, orbitals = integrals.shape
    blocks = screen.shape[0]
    grouped = integrals.reshape(blocks, aux_rows // blocks, local_pairs, orbitals)
    screened = jnp.where(screen[:, None, :, None] > 0, grouped, jnp.zeros_like(grouped)).reshape(
        aux_rows, local_pairs, orbitals
    )
    virtual = jnp.dot(
        screened.reshape(aux_rows * local_pairs, orbitals),
        virt_density,
        preferred_element_type=jnp.float32,
    ).astype(jnp.bfloat16).reshape(aux_rows, local_pairs, orbitals)
    got = lax.all_to_all(pack(jnp.stack([screened, virtual])), GROUP, 0, 0, tiled=True)
    own = unpack(got[:, :, :64])
    up = lax.ppermute(own, "y_hi", ring(1))
    down = lax.ppermute(own, "y_hi", ring(-1))
    core = lax.axis_index("core")
    far = lax.ppermute(jnp.where(core == 0, up, down), TALL, y_hop())
    spread = (jnp.arange(1024)[:, None] // 32 == jnp.arange(32)[None, :]).astype(jnp.bfloat16)
    tall = jnp.dot(spread, occ_density)
    full = lax.dot_general(tall, spread, (((1,), (1,)), ((), ())))
    same = jnp.arange(1024)[:, None] % 32 == jnp.arange(1024)[None, :] % 32
    mixer = jnp.where(same, full, jnp.zeros_like(full))
    occupied = jnp.dot(unpack(got[:, :, 64:]), mixer, preferred_element_type=jnp.float32)
    occupied = occupied.astype(jnp.bfloat16)
    near = lax.ppermute(occupied, WIDE, x_hop(True))
    back = lax.ppermute(occupied, WIDE, x_hop(False))
    beyond = lax.ppermute(near, WIDE, x_hop(True))
    mine = [occupied, near, beyond, back]
    other = lax.ppermute(jnp.stack(mine), "core", [(0, 1), (1, 0)])
    place = lax.axis_index("x_hi") * 2 + lax.axis_index("x_lo")
    where = jnp.stack([lax.axis_index("y_hi"), place, core]).astype(jnp.int32)
    tiles = multiply(where, [own, up, down, far], mine, other)
    got = lax.all_to_all(tiles, GROUP, 0, 0, tiled=True)
    total = jnp.sum(got.reshape(2, 2, 2, 8, 2, 2, 16, 128).astype(jnp.float32), axis=(1, 3))
    return total.transpose(5, 3, 0, 1, 2, 4).reshape(128, 256)


def solution(mesh):
    fine = Mesh(mesh.devices.reshape(2, 4, 2, 2, 8, 2), AUX + PAIR)
    placed = (P(AUX, PAIR, None), P(), P(), P(AUX, PAIR))

    return jax.shard_map(body, mesh=fine, in_specs=placed, out_specs=P(AUX, PAIR), check_vma=False)
```

time: 141 us -> 150 us (1.064)
  the two profiles are of different devices: /device:TPU:30 before, /device:TPU:6 now
where the time goes in v1:
time: 150 us; the launch traced here: 148 us
  starting transfers between devices  43.7 us (29%)
  waiting for transfers between devices  43.5 us (29%)
  blocking collectives  36.6 us (24%)
  local copies, waits for them, and re-layouts  10.5 us (7%)
  other arithmetic  7.41 us (5%)
  Pallas kernels  4.53 us (3%)
  matrix products  1.86 us (1%)
    all_to_all x1, blocking collectives, body(): got = lax.all_to_all(tiles, GROUP, 0, 0, tiled=True)  36.6 us
    all_to_all x1, waiting for transfers between devices, body(): lax.all_to_all(pack(jnp.stack([screened, virtual])), GROUP, 0, 0, tiled=T...  16.4 us
    all_to_all x1, starting transfers between devices, body(): lax.all_to_all(pack(jnp.stack([screened, virtual])), GROUP, 0, 0, tiled=T...  15.9 us
    ppermute x1, starting transfers between devices, body(): far = lax.ppermute(jnp.where(core == 0, up, down), TALL, y_hop())  9.95 us
    ppermute x1, waiting for transfers between devices, body(): far = lax.ppermute(jnp.where(core == 0, up, down), TALL, y_hop())  6.86 us
    ppermute x1, waiting for transfers between devices, body(): beyond = lax.ppermute(near, WIDE, x_hop(True))  6.3 us
    ppermute x1, waiting for transfers between devices, body(): up = lax.ppermute(own, 'y_hi', ring(1))  4.85 us
    ppermute x1, waiting for transfers between devices, body(): down = lax.ppermute(own, 'y_hi', ring(-1))  4.59 us
  transfers between devices with their start and end apart: 8, of which 6 were waited for; matrix products, arithmetic and copies ran while one was open for 1% of the time, Pallas kernels for 0%

profile of v1, /device:TPU:6, one launch (start us, length us, event | category | flops | bytes accessed | tf_op | source)
XLA Modules:
  0.0 148.3 jit_solution(15219434976551167680)
XLA Ops:
  0.0 0.0 copy-start
  0.0 1.1 reshape.131
  1.1 3.1 %reshape.130 = bf16[1,2,2,2,16,2,8,2,32]{8,7,6,5,4,3,2,1,0:T(2,128)(2,1)S(1)} reshape(bf16[128,2,512]{2,1,0:T(2,128)(2,1)} %param.4) | data formatting | bytes 524288 | tf_op jit(solution)/shard_map/reshape | solution.py:103
  4.2 0.7 broadcast_compare_fusion
  4.9 0.1 broadcast_in_dim.30
  5.0 0.0 copy-done
  5.0 0.3 convolution_convert_fusion
  5.4 0.6 stack.36
  6.0 1.2 copy.11
  7.1 1.1 broadcast_select_fusion
  8.3 3.5 %maximum_bitcast_fusion = bf16[2,2,2,8,2,16,2,2,32]{8,7,6,5,4,3,2,1,0:T(2,128)(2,1)S(1)} fusion(bf16[1,2,2,2,16,2,8,2,32]{8,5,0,4,3,6,2,7,1:T(2,128)(2,1)S(1)} %copy.11, bf16[1,2,2,2,16,2,8,2,32]{8,5,0,4,3,6,2,7,1:T(2,128)(2,1)S(1)} %broadcast_select_fusion), kind=kLoop, calls=%fused_computation.2 | loop fusion | flops 262144 | bytes 1048576 | tf_op jit(solution)/shard_map/transpose | solution.py:39
  11.8 0.0 copy-start.2
  11.8 1.7 %reshape.132 = bf16[128,16,128]{2,1,0:T(8,128)(2,1)} reshape(bf16[2,2,2,8,2,16,2,2,32]{8,7,6,5,4,3,2,1,0:T(2,128)(2,1)S(1)} %maximum_bitcast_fusion) | data formatting | bytes 1048576 | tf_op jit(solution)/shard_map/reshape | solution.py:39
  13.6 15.9 %all-to-all-start = ((bf16[128,16,128]{2,1,0:T(8,128)(2,1)}), bf16[128,16,128]{2,1,0:T(8,128)(2,1)S(1)}, u32[]{:S(2)}, u32[]{:S(2)}) async-start(bf16[128,16,128]{2,1,0:T(8,128)(2,1)} %reshape.132), calls=%async_computation | async-start | bytes 1048576 | tf_op jit(solution)/shard_map/all_to_all | solution.py:112
  29.5 0.0 copy-done.2
  29.5 0.3 fusion.7
  29.9 16.4 %all-to-all-done = bf16[128,16,128]{2,1,0:T(8,128)(2,1)S(1)} async-done(((bf16[128,16,128]{2,1,0:T(8,128)(2,1)}), bf16[128,16,128]{2,1,0:T(8,128)(2,1)S(1)}, u32[]{:S(2)}, u32[]{:S(2)}) %all-to-all-start) | async-done | bytes 524320 | tf_op jit(solution)/shard_map/all_to_all | solution.py:112
  46.3 1.0 fusion.21
  47.3 0.1 copy.18
  47.4 0.3 reshape.136
  47.7 1.2 fusion.5
  48.9 0.0 copy-start.1
  48.9 2.8 %collective-permute-start.3 = (bf16[128,1024]{1,0:T(8,128)(2,1)S(1)}, bf16[128,1024]{1,0:T(8,128)(2,1)S(1)}, u32[]{:S(2)}, u32[]{:S(2)}) collective-permute-start(bf16[128,1024]{1,0:T(8,128)(2,1)S(1)} %fusion.5), channel_id=1, source_target_pairs={{0,256},{16,273},{256,1},{272,16},{1,257},{17,272},{257,0},{273,17... | collective-permute-start | bytes 786440 | tf_op jit(solution)/shard_map/ppermute | solution.py:125
  51.8 3.1 %collective-permute-start.5 = (bf16[128,1024]{1,0:T(8,128)(2,1)S(1)}, bf16[128,1024]{1,0:T(8,128)(2,1)S(1)}, u32[]{:S(2)}, u32[]{:S(2)}) collective-permute-start(bf16[128,1024]{1,0:T(8,128)(2,1)S(1)} %fusion.5), channel_id=1, source_target_pairs={{0,257},{16,272},{256,0},{272,17},{1,256},{17,273},{257,1},{273,16... | collective-permute-start | bytes 786440 | tf_op jit(solution)/shard_map/ppermute | solution.py:126
  54.9 4.5 %collective-permute-done.3 = bf16[128,1024]{1,0:T(8,128)(2,1)S(1)} collective-permute-done((bf16[128,1024]{1,0:T(8,128)(2,1)S(1)}, bf16[128,1024]{1,0:T(8,128)(2,1)S(1)}, u32[]{:S(2)}, u32[]{:S(2)}) %collective-permute-start.3) | collective-permute-done | bytes 262176 | tf_op jit(solution)/shard_map/ppermute | solution.py:125
  59.4 1.9 %collective-permute-start.4 = (bf16[128,1024]{1,0:T(8,128)(2,1)S(1)}, bf16[128,1024]{1,0:T(8,128)(2,1)S(1)}, u32[]{:S(2)}, u32[]{:S(2)}) collective-permute-start(bf16[128,1024]{1,0:T(8,128)(2,1)S(1)} %collective-permute-done.3), channel_id=1, source_target_pairs={{0,256},{16,273},{256,1},{272,16},{1,257},{17,272},{257,0},{273,17... | collective-permute-start | bytes 786440 | tf_op jit(solution)/shard_map/ppermute | solution.py:127
  61.4 0.0 collective-permute-done.5
  61.4 6.3 %collective-permute-done.4 = bf16[128,1024]{1,0:T(8,128)(2,1)S(1)} collective-permute-done((bf16[128,1024]{1,0:T(8,128)(2,1)S(1)}, bf16[128,1024]{1,0:T(8,128)(2,1)S(1)}, u32[]{:S(2)}, u32[]{:S(2)}) %collective-permute-start.4) | collective-permute-done | bytes 262176 | tf_op jit(solution)/shard_map/ppermute | solution.py:127
  67.7 1.1 pad_maximum_fusion
  68.8 1.9 %collective-permute-start.6 = (bf16[4,128,1024]{2,1,0:T(8,128)(2,1)}, bf16[4,128,1024]{2,1,0:T(8,128)(2,1)S(1)}, u32[]{:S(2)}, u32[]{:S(2)}) collective-permute-start(bf16[4,128,1024]{2,1,0:T(8,128)(2,1)} %pad_maximum_fusion), channel_id=1, source_target_pairs={{0,16},{16,0},{1,17},{17,1},{2,18},{18,2},{3,19},{19,3},{4,20},{20... | collective-permute-start | bytes 3145736 | tf_op jit(solution)/shard_map/ppermute | solution.py:129
  70.7 0.0 copy-done.1
  70.7 0.1 copy.12
  70.8 0.3 reshape.134.refs_0_
  71.2 4.5 %collective-permute-start = (bf16[128,1024]{1,0:T(8,128)(2,1)S(1)}, bf16[128,1024]{1,0:T(8,128)(2,1)S(1)}, u32[]{:S(2)}, u32[]{:S(2)}) collective-permute-start(bf16[128,1024]{1,0:T(8,128)(2,1)S(1)} %reshape.134.refs_0_), channel_id=1, source_target_pairs={{0,64},{64,128},{128,192},{192,0},{1,65},{65,129},{129,193},{193,1... | collective-permute-start | bytes 786440 | tf_op jit(solution)/shard_map/ppermute | solution.py:114
  75.7 3.5 %collective-permute-start.1 = (bf16[128,1024]{1,0:T(8,128)(2,1)S(1)}, bf16[128,1024]{1,0:T(8,128)(2,1)S(1)}, u32[]{:S(2)}, u32[]{:S(2)}) collective-permute-start(bf16[128,1024]{1,0:T(8,128)(2,1)S(1)} %reshape.134.refs_0_), channel_id=1, source_target_pairs={{0,192},{64,0},{128,64},{192,128},{1,193},{65,1},{129,65},{193,129... | collective-permute-start | bytes 786440 | tf_op jit(solution)/shard_map/ppermute | solution.py:115
  79.2 4.9 %collective-permute-done.refs_1_ = bf16[128,1024]{1,0:T(8,128)(2,1)S(1)} collective-permute-done((bf16[128,1024]{1,0:T(8,128)(2,1)S(1)}, bf16[128,1024]{1,0:T(8,128)(2,1)S(1)}, u32[]{:S(2)}, u32[]{:S(2)}) %collective-permute-start) | collective-permute-done | bytes 262176 | tf_op jit(solution)/shard_map/ppermute | solution.py:114
  84.0 4.6 %collective-permute-done.1.refs_2_ = bf16[128,1024]{1,0:T(8,128)(2,1)S(1)} collective-permute-done((bf16[128,1024]{1,0:T(8,128)(2,1)S(1)}, bf16[128,1024]{1,0:T(8,128)(2,1)S(1)}, u32[]{:S(2)}, u32[]{:S(2)}) %collective-permute-start.1) | collective-permute-done | bytes 262176 | tf_op jit(solution)/shard_map/ppermute | solution.py:115
  88.6 0.7 broadcast_select_fusion.1
  89.3 10.0 %collective-permute-start.2 = (bf16[128,1024]{1,0:T(8,128)(2,1)}, bf16[128,1024]{1,0:T(8,128)(2,1)}, u32[]{:S(2)}, u32[]{:S(2)}) collective-permute-start(bf16[128,1024]{1,0:T(8,128)(2,1)} %broadcast_select_fusion.1), channel_id=1, source_target_pairs={{0,64},{16,208},{64,128},{80,16},{128,192},{144,80},{192,0},{208,1... | collective-permute-start | bytes 786440 | tf_op jit(solution)/shard_map/ppermute | solution.py:117
  99.3 0.1 pad_add_fusion.where_ref
  99.4 6.9 %collective-permute-done.2.refs_3_ = bf16[128,1024]{1,0:T(8,128)(2,1)} collective-permute-done((bf16[128,1024]{1,0:T(8,128)(2,1)}, bf16[128,1024]{1,0:T(8,128)(2,1)}, u32[]{:S(2)}, u32[]{:S(2)}) %collective-permute-start.2) | collective-permute-done | bytes 262176 | tf_op jit(solution)/shard_map/ppermute | solution.py:117
  106.2 0.0 collective-permute-done.6
  106.2 4.5 %shard_map.46 = bf16[128,32,128]{2,1,0:T(8,128)(2,1)S(1)} custom-call(s32[3]{0:T(128)S(1)} %pad_add_fusion.where_ref, bf16[128,1024]{1,0:T(8,128)(2,1)S(1)} %reshape.134.refs_0_, bf16[128,1024]{1,0:T(8,128)(2,1)S(1)} %collective-permute-done.refs_1_, bf16[128,1024]{1,0:T(8,128)(2,1)S(1)} %collective-permute-done.1.refs_2_, ...), custom_call_target="tpu_custom_call" | custom-call | flops 1073741824 | bytes 4194304 | tf_op jit(solution)/shard_map/pallas_call | solution.py:85
  110.8 36.6 %all_to_all.10 = bf16[128,32,128]{2,1,0:T(8,128)(2,1)S(1)} all-to-all(bf16[128,32,128]{2,1,0:T(8,128)(2,1)S(1)} %shard_map.46), channel_id=1, replica_groups=mesh['x_lo'=2,'y_hi'=4,'y_lo'=2,'core'=2,'z'=8,'x_hi'=2] {'x_lo','y_lo',..., dimensions={0} | all-to-all | bytes 2097152 | tf_op jit(solution)/shard_map/all_to_all | solution.py:133
  147.4 0.2 convert_reduce_fusion
  147.6 0.8 copy.15
  (3 shorter events, 0.0 us)
Async XLA Ops:
  0.0 5.0 %copy-start = (bf16[512,512]{1,0:T(8,128)(2,1)S(1)}, bf16[512,512]{1,0:T(8,128)(2,1)}, u32[]{:S(2)}) copy-start(bf16[512,512]{1,0:T(8,128)(2,1)} %param.6) | copy-start | bytes 1572868
  11.8 17.7 %copy-start.2 = (bf16[32,32]{1,0:T(8,128)(2,1)S(1)}, bf16[32,32]{1,0:T(8,128)(2,1)}, u32[]{:S(2)}) copy-start(bf16[32,32]{1,0:T(8,128)(2,1)} %param.5) | copy-start | bytes 6148
  13.6 32.7 %all-to-all-start = ((bf16[128,16,128]{2,1,0:T(8,128)(2,1)}), bf16[128,16,128]{2,1,0:T(8,128)(2,1)S(1)}, u32[]{:S(2)}, u32[]{:S(2)}) async-start(bf16[128,16,128]{2,1,0:T(8,128)(2,1)} %reshape.132), calls=%async_computation | async-start | bytes 1048576 | tf_op jit(solution)/shard_map/all_to_all | solution.py:112
  48.9 21.8 %copy-start.1 = (bf16[128,16,64]{2,1,0:T(8,128)(2,1)S(1)}, bf16[128,16,64]{2,1,0:T(8,128)(2,1)}, u32[]{:S(2)}) copy-start(bf16[128,16,64]{2,1,0:T(8,128)(2,1)} %get-tuple-element.6) | copy-start | bytes 786436
  48.9 10.5 %collective-permute-start.3 = (bf16[128,1024]{1,0:T(8,128)(2,1)S(1)}, bf16[128,1024]{1,0:T(8,128)(2,1)S(1)}, u32[]{:S(2)}, u32[]{:S(2)}) collective-permute-start(bf16[128,1024]{1,0:T(8,128)(2,1)S(1)} %fusion.5), channel_id=1, source_target_pairs={{0,256},{16,273},{256,1},{272,16},{1,257},{17,272},{257,0},{273,17... | collective-permute-start | bytes 786440 | tf_op jit(solution)/shard_map/ppermute | solution.py:125
  51.8 9.6 %collective-permute-start.5 = (bf16[128,1024]{1,0:T(8,128)(2,1)S(1)}, bf16[128,1024]{1,0:T(8,128)(2,1)S(1)}, u32[]{:S(2)}, u32[]{:S(2)}) collective-permute-start(bf16[128,1024]{1,0:T(8,128)(2,1)S(1)} %fusion.5), channel_id=1, source_target_pairs={{0,257},{16,272},{256,0},{272,17},{1,256},{17,273},{257,1},{273,16... | collective-permute-start | bytes 786440 | tf_op jit(solution)/shard_map/ppermute | solution.py:126
  59.4 8.3 %collective-permute-start.4 = (bf16[128,1024]{1,0:T(8,128)(2,1)S(1)}, bf16[128,1024]{1,0:T(8,128)(2,1)S(1)}, u32[]{:S(2)}, u32[]{:S(2)}) collective-permute-start(bf16[128,1024]{1,0:T(8,128)(2,1)S(1)} %collective-permute-done.3), channel_id=1, source_target_pairs={{0,256},{16,273},{256,1},{272,16},{1,257},{17,272},{257,0},{273,17... | collective-permute-start | bytes 786440 | tf_op jit(solution)/shard_map/ppermute | solution.py:127
  68.8 37.5 %collective-permute-start.6 = (bf16[4,128,1024]{2,1,0:T(8,128)(2,1)}, bf16[4,128,1024]{2,1,0:T(8,128)(2,1)S(1)}, u32[]{:S(2)}, u32[]{:S(2)}) collective-permute-start(bf16[4,128,1024]{2,1,0:T(8,128)(2,1)} %pad_maximum_fusion), channel_id=1, source_target_pairs={{0,16},{16,0},{1,17},{17,1},{2,18},{18,2},{3,19},{19,3},{4,20},{20... | collective-permute-start | bytes 3145736 | tf_op jit(solution)/shard_map/ppermute | solution.py:129
  71.2 12.8 %collective-permute-start = (bf16[128,1024]{1,0:T(8,128)(2,1)S(1)}, bf16[128,1024]{1,0:T(8,128)(2,1)S(1)}, u32[]{:S(2)}, u32[]{:S(2)}) collective-permute-start(bf16[128,1024]{1,0:T(8,128)(2,1)S(1)} %reshape.134.refs_0_), channel_id=1, source_target_pairs={{0,64},{64,128},{128,192},{192,0},{1,65},{65,129},{129,193},{193,1... | collective-permute-start | bytes 786440 | tf_op jit(solution)/shard_map/ppermute | solution.py:114
  75.7 12.9 %collective-permute-start.1 = (bf16[128,1024]{1,0:T(8,128)(2,1)S(1)}, bf16[128,1024]{1,0:T(8,128)(2,1)S(1)}, u32[]{:S(2)}, u32[]{:S(2)}) collective-permute-start(bf16[128,1024]{1,0:T(8,128)(2,1)S(1)} %reshape.134.refs_0_), channel_id=1, source_target_pairs={{0,192},{64,0},{128,64},{192,128},{1,193},{65,1},{129,65},{193,129... | collective-permute-start | bytes 786440 | tf_op jit(solution)/shard_map/ppermute | solution.py:115
  89.3 16.9 %collective-permute-start.2 = (bf16[128,1024]{1,0:T(8,128)(2,1)}, bf16[128,1024]{1,0:T(8,128)(2,1)}, u32[]{:S(2)}, u32[]{:S(2)}) collective-permute-start(bf16[128,1024]{1,0:T(8,128)(2,1)} %broadcast_select_fusion.1), channel_id=1, source_target_pairs={{0,64},{16,208},{64,128},{80,16},{128,192},{144,80},{192,0},{208,1... | collective-permute-start | bytes 786440 | tf_op jit(solution)/shard_map/ppermute | solution.py:117

commit v2 on v0

--- a/solution.py
+++ b/solution.py
@@ -14,6 +14,10 @@
 
 def ring(step):
     return [(y, (y + step) % 8) for y in range(8)]
+
+
+def y_hop(steps):
+    return [(y * 2 + c, (y + steps * (1 - 2 * c)) % 8 * 2 + c) for y in range(8) for c in range(2)]
 
 
 def wide_index(place, core):
@@ -39,7 +43,7 @@
 
 
 def multiply_kernel(where_ref, *refs):
-    columns, mine, other, (out_ref, left, right, done) = refs[:9], refs[9:13], refs[13], refs[14:]
+    columns, mine, other, (out_ref, left, right, done) = refs[:8], refs[8:12], refs[12], refs[13:]
     y, place, core = where_ref[0], where_ref[1], where_ref[2]
     copies = []
 
@@ -47,12 +51,9 @@
         copies.append(pltpu.make_async_copy(source, target, done.at[len(copies)]))
         copies[-1].start()
 
-    for i, steps in enumerate((0, 1, 2, 3, -1, -2, -3)):
+    for i, steps in enumerate((0, 1, 2, 3, -1, -2, -3, 4)):
         at = lax.rem(y - steps + 8, 8)
         bring(columns[i], left.at[pl.ds(pl.multiple_of(at * 64, 64), 64), :])
-    at = lax.rem(y + 4, 8)
-    bring(columns[7], left.at[pl.ds(pl.multiple_of(at * 64, 32), 32), :])
-    bring(columns[8], left.at[pl.ds(pl.multiple_of(at * 64 + 32, 32), 32), :])
     sign = 1 - 2 * core
     for i, steps in enumerate((0, 1, 2, -1)):
         for near in range(2):
@@ -83,14 +84,14 @@
     return pl.pallas_call(
         multiply_kernel,
         out_shape=jax.ShapeDtypeStruct((64, 32, 128), jnp.bfloat16),
-        in_specs=[pl.BlockSpec(memory_space=pltpu.SMEM)] + [pl.BlockSpec(memory_space=pl.ANY)] * 14,
+        in_specs=[pl.BlockSpec(memory_space=pltpu.SMEM)] + [pl.BlockSpec(memory_space=pl.ANY)] * 13,
         out_specs=pl.BlockSpec(memory_space=pltpu.VMEM),
         scratch_shapes=[
             pltpu.VMEM((512, 2048), jnp.bfloat16),
             pltpu.VMEM((4, 128, 2048), jnp.bfloat16),
-            pltpu.SemaphoreType.DMA((17,)),
+            pltpu.SemaphoreType.DMA((16,)),
         ],
-        compiler_params=pltpu.CompilerParams(vmem_limit_bytes=16 * 1024 * 1024),
+        compiler_params=pltpu.CompilerParams(vmem_limit_bytes=20 * 1024 * 1024),
         cost_estimate=pl.CostEstimate(flops=2 * 512 * 512 * 2048, bytes_accessed=4 << 20, transcendentals=0),
     )(where, *columns, *mine, other.reshape(4, 4, 16, 2048))
 
@@ -110,25 +111,25 @@
     both = jnp.concatenate([pack(screened), pack(virtual)], axis=1)
     got = lax.all_to_all(both, PLANE, 0, 0, tiled=True)
     own = unpack(got[:, :16])
+    core = lax.axis_index("core")
     up1 = lax.ppermute(own, "y", ring(1))
     down1 = lax.ppermute(own, "y", ring(-1))
-    up2 = lax.ppermute(up1, "y", ring(1))
-    down2 = lax.ppermute(down1, "y", ring(-1))
+    up2 = lax.ppermute(own, "y", ring(2))
+    down2 = lax.ppermute(own, "y", ring(-2))
     up3 = lax.ppermute(up2, "y", ring(1))
     down3 = lax.ppermute(down2, "y", ring(-1))
-    up4 = lax.ppermute(up3[:32], "y", ring(1))
-    down4 = lax.ppermute(down3[32:], "y", ring(-1))
-    columns = [own, up1, up2, up3, down1, down2, down3, up4, down4]
+    far = lax.ppermute(jnp.where(core == 0, up2, down2), ("y", "core"), y_hop(2))
+    columns = [own, up1, up2, up3, down1, down2, down3, far]
     virt_rows = unpack(got[:, 16:]).reshape(64, 32, 64)
     occupied = jnp.einsum("pms,ml->pls", virt_rows, occ_density, preferred_element_type=jnp.float32)
-    occupied = occupied.astype(jnp.bfloat16).reshape(64, 2048)
+    occupied = lax.optimization_barrier(occupied.astype(jnp.bfloat16).reshape(64, 2048))
     near = lax.ppermute(occupied, WIDE, x_hop(True))
     back = lax.ppermute(occupied, WIDE, x_hop(False))
     far = lax.ppermute(near, WIDE, x_hop(True))
     mine = [occupied, near, far, back]
     other = lax.ppermute(jnp.stack(mine), "core", [(0, 1), (1, 0)])
     place = lax.axis_index("x_hi") * 2 + lax.axis_index("x_lo")
-    where = jnp.stack([lax.axis_index("y"), place, lax.axis_index("core")]).astype(jnp.int32)
+    where = jnp.stack([lax.axis_index("y"), place, core]).astype(jnp.int32)
     tiles = multiply(where, columns, mine, other)
     got = lax.all_to_all(tiles, PLANE, 0, 0, tiled=True)
     total = jnp.sum(got.reshape(2, 2, 8, 2, 2, 16, 128).astype(jnp.float32), axis=2)

time: 141 us -> 132 us (0.936)
  the two profiles are of different devices: /device:TPU:30 before, /device:TPU:6 now
where the time goes in v2:
time: 132 us; the launch traced here: 131 us
  blocking collectives  56.2 us (43%)
  starting transfers between devices  37.9 us (29%)
  waiting for transfers between devices  22.9 us (17%)
  local copies, waits for them, and re-layouts  7.06 us (5%)
  Pallas kernels  3.25 us (2%)
  other arithmetic  2.61 us (2%)
    all_to_all x1, blocking collectives, body(): got = lax.all_to_all(both, PLANE, 0, 0, tiled=True)  32.2 us
    all_to_all x1, blocking collectives, body(): got = lax.all_to_all(tiles, PLANE, 0, 0, tiled=True)  24.1 us
    ppermute x1, waiting for transfers between devices, body(): down2 = lax.ppermute(own, 'y', ring(-2))  6.47 us
    ppermute x1, waiting for transfers between devices, body(): far = lax.ppermute(near, WIDE, x_hop(True))  6.33 us
    ppermute x1, starting transfers between devices, body(): lax.ppermute(jnp.where(core == 0, up2, down2), ('y', 'core'), y_hop(2))  6.09 us
    ppermute x1, waiting for transfers between devices, body(): near = lax.ppermute(occupied, WIDE, x_hop(True))  5.2 us
    ppermute x1, starting transfers between devices, body(): down3 = lax.ppermute(down2, 'y', ring(-1))  5.12 us
    ppermute x1, starting transfers between devices, body(): up2 = lax.ppermute(own, 'y', ring(2))  4.5 us
  transfers between devices with their start and end apart: 11, of which 6 were waited for; matrix products, arithmetic and copies ran while one was open for 1% of the time, Pallas kernels for 0%

profile of v2, /device:TPU:6, one launch (start us, length us, event | category | flops | bytes accessed | tf_op | source)
XLA Modules:
  0.0 131.0 jit_solution(9695398877753635620)
XLA Ops:
  0.0 1.1 reshape.51
  1.1 0.0 copy-start.5
  1.2 0.3 reshape.49
  1.5 0.3 copy-done.5
  1.8 0.1 broadcast_in_dim.23
  2.0 0.3 convolution_convert_fusion.1
  2.4 0.3 reshape_reshape.8
  2.6 0.5 copy.25
  3.2 0.2 reshape.52
  3.4 0.6 fusion.1
  4.0 0.2 reshape.50
  4.3 32.2 %all_to_all.10 = bf16[64,32,128]{2,1,0:T(8,128)(2,1)S(1)} all-to-all(bf16[64,32,128]{2,1,0:T(8,128)(2,1)S(1)} %pad_maximum_fusion.1), channel_id=1, replica_groups=mesh['x_lo'=2,'y'=8,'core'=2,'z'=8,'x_hi'=2] {'x_lo','core','z','x_hi'}, dimensions={0} | all-to-all | bytes 1048576 | tf_op jit(solution)/shard_map/all_to_all | solution.py:112
  36.5 0.1 copy.15
  36.6 0.0 copy-start.4
  36.6 0.2 reshape_reshape.9
  36.9 0.4 copy-done.4
  37.3 0.3 fusion
  37.6 0.5 reshape.56
  38.1 2.2 %collective-permute-start.7 = (bf16[64,2048]{1,0:T(8,128)(2,1)S(1)}, bf16[64,2048]{1,0:T(8,128)(2,1)S(1)}, u32[]{:S(2)}, u32[]{:S(2)}) collective-permute-start(bf16[64,2048]{1,0:T(8,128)(2,1)S(1)} %reshape.56), channel_id=1, source_target_pairs={{0,256},{16,273},{256,1},{272,16},{1,257},{17,272},{257,0},{273,17... | collective-permute-start | bytes 786440 | tf_op jit(solution)/shard_map/ppermute | solution.py:126
  40.3 3.6 %collective-permute-start.9 = (bf16[64,2048]{1,0:T(8,128)(2,1)S(1)}, bf16[64,2048]{1,0:T(8,128)(2,1)S(1)}, u32[]{:S(2)}, u32[]{:S(2)}) collective-permute-start(bf16[64,2048]{1,0:T(8,128)(2,1)S(1)} %reshape.56), channel_id=1, source_target_pairs={{0,257},{16,272},{256,0},{272,17},{1,256},{17,273},{257,1},{273,16... | collective-permute-start | bytes 786440 | tf_op jit(solution)/shard_map/ppermute | solution.py:127
  44.0 5.2 %collective-permute-done.7 = bf16[64,2048]{1,0:T(8,128)(2,1)S(1)} collective-permute-done((bf16[64,2048]{1,0:T(8,128)(2,1)S(1)}, bf16[64,2048]{1,0:T(8,128)(2,1)S(1)}, u32[]{:S(2)}, u32[]{:S(2)}) %collective-permute-start.7) | collective-permute-done | bytes 262176 | tf_op jit(solution)/shard_map/ppermute | solution.py:126
  49.1 1.9 %collective-permute-start.8 = (bf16[64,2048]{1,0:T(8,128)(2,1)S(1)}, bf16[64,2048]{1,0:T(8,128)(2,1)S(1)}, u32[]{:S(2)}, u32[]{:S(2)}) collective-permute-start(bf16[64,2048]{1,0:T(8,128)(2,1)S(1)} %collective-permute-done.7), channel_id=1, source_target_pairs={{0,256},{16,273},{256,1},{272,16},{1,257},{17,272},{257,0},{273,17... | collective-permute-start | bytes 786440 | tf_op jit(solution)/shard_map/ppermute | solution.py:128
  51.1 6.3 %collective-permute-done.8 = bf16[64,2048]{1,0:T(8,128)(2,1)S(1)} collective-permute-done((bf16[64,2048]{1,0:T(8,128)(2,1)S(1)}, bf16[64,2048]{1,0:T(8,128)(2,1)S(1)}, u32[]{:S(2)}, u32[]{:S(2)}) %collective-permute-start.8) | collective-permute-done | bytes 262176 | tf_op jit(solution)/shard_map/ppermute | solution.py:128
  57.4 1.1 pad_maximum_fusion
  58.5 1.9 %collective-permute-start.10 = (bf16[4,64,2048]{2,1,0:T(8,128)(2,1)}, bf16[4,64,2048]{2,1,0:T(8,128)(2,1)S(1)}, u32[]{:S(2)}, u32[]{:S(2)}) collective-permute-start(bf16[4,64,2048]{2,1,0:T(8,128)(2,1)} %pad_maximum_fusion), channel_id=1, source_target_pairs={{0,16},{16,0},{1,17},{17,1},{2,18},{18,2},{3,19},{19,3},{4,20},{20... | collective-permute-start | bytes 3145736 | tf_op jit(solution)/shard_map/ppermute | solution.py:130
  60.4 0.1 copy.14
  60.5 0.1 copy.26
  60.6 4.5 %collective-permute-start.1 = (bf16[64,2048]{1,0:T(8,128)(2,1)S(1)}, bf16[64,2048]{1,0:T(8,128)(2,1)S(1)}, u32[]{:S(2)}, u32[]{:S(2)}) collective-permute-start(bf16[64,2048]{1,0:T(8,128)(2,1)S(1)} %bitcast.44), channel_id=1, source_target_pairs={{0,64},{32,96},{64,128},{96,160},{128,192},{160,224},{192,0},{224,... | collective-permute-start | bytes 786440 | tf_op jit(solution)/shard_map/ppermute | solution.py:117
  65.1 3.6 %collective-permute-start.4 = (bf16[64,2048]{1,0:T(8,128)(2,1)S(1)}, bf16[64,2048]{1,0:T(8,128)(2,1)S(1)}, u32[]{:S(2)}, u32[]{:S(2)}) collective-permute-start(bf16[64,2048]{1,0:T(8,128)(2,1)S(1)} %bitcast.45), channel_id=1, source_target_pairs={{0,192},{32,224},{64,0},{96,32},{128,64},{160,96},{192,128},{224,1... | collective-permute-start | bytes 786440 | tf_op jit(solution)/shard_map/ppermute | solution.py:118
  68.7 3.3 %collective-permute-start = (bf16[64,2048]{1,0:T(8,128)(2,1)S(1)}, bf16[64,2048]{1,0:T(8,128)(2,1)S(1)}, u32[]{:S(2)}, u32[]{:S(2)}) collective-permute-start(bf16[64,2048]{1,0:T(8,128)(2,1)S(1)} %bitcast.46), channel_id=1, source_target_pairs={{0,32},{32,64},{64,96},{96,128},{128,160},{160,192},{192,224},{224... | collective-permute-start | bytes 786440 | tf_op jit(solution)/shard_map/ppermute | solution.py:115
  72.1 3.7 %collective-permute-start.3 = (bf16[64,2048]{1,0:T(8,128)(2,1)S(1)}, bf16[64,2048]{1,0:T(8,128)(2,1)}, u32[]{:S(2)}, u32[]{:S(2)}) collective-permute-start(bf16[64,2048]{1,0:T(8,128)(2,1)S(1)} %bitcast.47), channel_id=1, source_target_pairs={{0,224},{32,0},{64,32},{96,64},{128,96},{160,128},{192,160},{224,1... | collective-permute-start | bytes 786440 | tf_op jit(solution)/shard_map/ppermute | solution.py:116
  75.8 1.1 collective-permute-done.1.refs_2_
  76.9 6.5 %collective-permute-done.4.refs_5_ = bf16[64,2048]{1,0:T(8,128)(2,1)S(1)} collective-permute-done((bf16[64,2048]{1,0:T(8,128)(2,1)S(1)}, bf16[64,2048]{1,0:T(8,128)(2,1)S(1)}, u32[]{:S(2)}, u32[]{:S(2)}) %collective-permute-start.4) | collective-permute-done | bytes 262176 | tf_op jit(solution)/shard_map/ppermute | solution.py:118
  83.4 0.7 broadcast_select_fusion.1
  84.1 6.1 %collective-permute-start.6 = (bf16[64,2048]{1,0:T(8,128)(2,1)}, bf16[64,2048]{1,0:T(8,128)(2,1)}, u32[]{:S(2)}, u32[]{:S(2)}) collective-permute-start(bf16[64,2048]{1,0:T(8,128)(2,1)} %broadcast_select_fusion.1), channel_id=1, source_target_pairs={{0,64},{16,208},{32,96},{48,240},{64,128},{80,16},{96,160},{112,48... | collective-permute-start | bytes 786440 | tf_op jit(solution)/shard_map/ppermute | solution.py:121
  90.2 1.9 %collective-permute-start.2 = (bf16[64,2048]{1,0:T(8,128)(2,1)S(1)}, bf16[64,2048]{1,0:T(8,128)(2,1)}, u32[]{:S(2)}, u32[]{:S(2)}) collective-permute-start(bf16[64,2048]{1,0:T(8,128)(2,1)S(1)} %collective-permute-done.1.refs_2_), channel_id=1, source_target_pairs={{0,32},{32,64},{64,96},{96,128},{128,160},{160,192},{192,224},{224... | collective-permute-start | bytes 786440 | tf_op jit(solution)/shard_map/ppermute | solution.py:119
  92.1 0.0 collective-permute-done.refs_1_
  92.1 0.7 copy-done.1
  92.8 5.1 %collective-permute-start.5 = (bf16[64,2048]{1,0:T(8,128)(2,1)S(1)}, bf16[64,2048]{1,0:T(8,128)(2,1)}, u32[]{:S(2)}, u32[]{:S(2)}) collective-permute-start(bf16[64,2048]{1,0:T(8,128)(2,1)S(1)} %collective-permute-done.4.refs_5_), channel_id=1, source_target_pairs={{0,224},{32,0},{64,32},{96,64},{128,96},{160,128},{192,160},{224,1... | collective-permute-start | bytes 786440 | tf_op jit(solution)/shard_map/ppermute | solution.py:120
  98.0 0.1 pad_add_fusion.where_ref
  98.1 0.0 collective-permute-done.6.refs_7_
  98.1 3.0 %collective-permute-done.2.refs_3_ = bf16[64,2048]{1,0:T(8,128)(2,1)} collective-permute-done((bf16[64,2048]{1,0:T(8,128)(2,1)S(1)}, bf16[64,2048]{1,0:T(8,128)(2,1)}, u32[]{:S(2)}, u32[]{:S(2)}) %collective-permute-start.2) | collective-permute-done | bytes 262176 | tf_op jit(solution)/shard_map/ppermute | solution.py:119
  101.1 0.7 collective-permute-done.5.refs_6_
  101.8 0.9 copy-done.2
  102.8 3.2 %shard_map.46 = bf16[64,32,128]{2,1,0:T(8,128)(2,1)S(1)} custom-call(s32[3]{0:T(128)S(1)} %pad_add_fusion.where_ref, bf16[64,2048]{1,0:T(8,128)(2,1)S(1)} %bitcast.48, bf16[64,2048]{1,0:T(8,128)(2,1)S(1)} %copy-done.2, bf16[64,2048]{1,0:T(8,128)(2,1)S(1)} %collective-permute-done.1.refs_2_, bf16[64,2048]{1,0:T(8,128)(2,1)} %collective-permute-done.2.refs_3_, ...), custom_call_target="tpu_custom_call" | custom-call | flops 1073741824 | bytes 4194304 | tf_op jit(solution)/shard_map/pallas_call | solution.py:84
  106.0 24.1 %all_to_all.11 = bf16[64,32,128]{2,1,0:T(8,128)(2,1)S(1)} all-to-all(bf16[64,32,128]{2,1,0:T(8,128)(2,1)S(1)} %shard_map.46), channel_id=1, replica_groups=mesh['x_lo'=2,'y'=8,'core'=2,'z'=8,'x_hi'=2] {'x_lo','core','z','x_hi'}, dimensions={0} | all-to-all | bytes 1048576 | tf_op jit(solution)/shard_map/all_to_all | solution.py:134
  130.1 0.1 convert_reduce_fusion
  130.2 0.8 copy.18
  (14 shorter events, 0.1 us)
Async XLA Ops:
  0.0 2.0 %copy-start = (bf16[512,512]{1,0:T(8,128)(2,1)S(1)}, bf16[512,512]{1,0:T(8,128)(2,1)}, u32[]{:S(2)}) copy-start(bf16[512,512]{1,0:T(8,128)(2,1)} %param.6) | copy-start | bytes 1572868
  0.0 1.1 copy-start.3
  1.1 0.7 copy-start.5
  36.6 0.7 copy-start.4
  38.1 11.1 %collective-permute-start.7 = (bf16[64,2048]{1,0:T(8,128)(2,1)S(1)}, bf16[64,2048]{1,0:T(8,128)(2,1)S(1)}, u32[]{:S(2)}, u32[]{:S(2)}) collective-permute-start(bf16[64,2048]{1,0:T(8,128)(2,1)S(1)} %reshape.56), channel_id=1, source_target_pairs={{0,256},{16,273},{256,1},{272,16},{1,257},{17,272},{257,0},{273,17... | collective-permute-start | bytes 786440 | tf_op jit(solution)/shard_map/ppermute | solution.py:126
  40.3 10.7 %collective-permute-start.9 = (bf16[64,2048]{1,0:T(8,128)(2,1)S(1)}, bf16[64,2048]{1,0:T(8,128)(2,1)S(1)}, u32[]{:S(2)}, u32[]{:S(2)}) collective-permute-start(bf16[64,2048]{1,0:T(8,128)(2,1)S(1)} %reshape.56), channel_id=1, source_target_pairs={{0,257},{16,272},{256,0},{272,17},{1,256},{17,273},{257,1},{273,16... | collective-permute-start | bytes 786440 | tf_op jit(solution)/shard_map/ppermute | solution.py:127
  49.1 8.3 %collective-permute-start.8 = (bf16[64,2048]{1,0:T(8,128)(2,1)S(1)}, bf16[64,2048]{1,0:T(8,128)(2,1)S(1)}, u32[]{:S(2)}, u32[]{:S(2)}) collective-permute-start(bf16[64,2048]{1,0:T(8,128)(2,1)S(1)} %collective-permute-done.7), channel_id=1, source_target_pairs={{0,256},{16,273},{256,1},{272,16},{1,257},{17,272},{257,0},{273,17... | collective-permute-start | bytes 786440 | tf_op jit(solution)/shard_map/ppermute | solution.py:128
  58.5 43.3 %collective-permute-start.10 = (bf16[4,64,2048]{2,1,0:T(8,128)(2,1)}, bf16[4,64,2048]{2,1,0:T(8,128)(2,1)S(1)}, u32[]{:S(2)}, u32[]{:S(2)}) collective-permute-start(bf16[4,64,2048]{2,1,0:T(8,128)(2,1)} %pad_maximum_fusion), channel_id=1, source_target_pairs={{0,16},{16,0},{1,17},{17,1},{2,18},{18,2},{3,19},{19,3},{4,20},{20... | collective-permute-start | bytes 3145736 | tf_op jit(solution)/shard_map/ppermute | solution.py:130
  60.6 16.3 %collective-permute-start.1 = (bf16[64,2048]{1,0:T(8,128)(2,1)S(1)}, bf16[64,2048]{1,0:T(8,128)(2,1)S(1)}, u32[]{:S(2)}, u32[]{:S(2)}) collective-permute-start(bf16[64,2048]{1,0:T(8,128)(2,1)S(1)} %bitcast.44), channel_id=1, source_target_pairs={{0,64},{32,96},{64,128},{96,160},{128,192},{160,224},{192,0},{224,... | collective-permute-start | bytes 786440 | tf_op jit(solution)/shard_map/ppermute | solution.py:117
  65.1 18.3 %collective-permute-start.4 = (bf16[64,2048]{1,0:T(8,128)(2,1)S(1)}, bf16[64,2048]{1,0:T(8,128)(2,1)S(1)}, u32[]{:S(2)}, u32[]{:S(2)}) collective-permute-start(bf16[64,2048]{1,0:T(8,128)(2,1)S(1)} %bitcast.45), channel_id=1, source_target_pairs={{0,192},{32,224},{64,0},{96,32},{128,64},{160,96},{192,128},{224,1... | collective-permute-start | bytes 786440 | tf_op jit(solution)/shard_map/ppermute | solution.py:118
  68.7 23.4 %collective-permute-start = (bf16[64,2048]{1,0:T(8,128)(2,1)S(1)}, bf16[64,2048]{1,0:T(8,128)(2,1)S(1)}, u32[]{:S(2)}, u32[]{:S(2)}) collective-permute-start(bf16[64,2048]{1,0:T(8,128)(2,1)S(1)} %bitcast.46), channel_id=1, source_target_pairs={{0,32},{32,64},{64,96},{96,128},{128,160},{160,192},{192,224},{224... | collective-permute-start | bytes 786440 | tf_op jit(solution)/shard_map/ppermute | solution.py:115
  72.1 26.0 %collective-permute-start.3 = (bf16[64,2048]{1,0:T(8,128)(2,1)S(1)}, bf16[64,2048]{1,0:T(8,128)(2,1)}, u32[]{:S(2)}, u32[]{:S(2)}) collective-permute-start(bf16[64,2048]{1,0:T(8,128)(2,1)S(1)} %bitcast.47), channel_id=1, source_target_pairs={{0,224},{32,0},{64,32},{96,64},{128,96},{160,128},{192,160},{224,1... | collective-permute-start | bytes 786440 | tf_op jit(solution)/shard_map/ppermute | solution.py:116
  84.1 14.0 %collective-permute-start.6 = (bf16[64,2048]{1,0:T(8,128)(2,1)}, bf16[64,2048]{1,0:T(8,128)(2,1)}, u32[]{:S(2)}, u32[]{:S(2)}) collective-permute-start(bf16[64,2048]{1,0:T(8,128)(2,1)} %broadcast_select_fusion.1), channel_id=1, source_target_pairs={{0,64},{16,208},{32,96},{48,240},{64,128},{80,16},{96,160},{112,48... | collective-permute-start | bytes 786440 | tf_op jit(solution)/shard_map/ppermute | solution.py:121
  90.2 10.9 %collective-permute-start.2 = (bf16[64,2048]{1,0:T(8,128)(2,1)S(1)}, bf16[64,2048]{1,0:T(8,128)(2,1)}, u32[]{:S(2)}, u32[]{:S(2)}) collective-permute-start(bf16[64,2048]{1,0:T(8,128)(2,1)S(1)} %collective-permute-done.1.refs_2_), channel_id=1, source_target_pairs={{0,32},{32,64},{64,96},{96,128},{128,160},{160,192},{192,224},{224... | collective-permute-start | bytes 786440 | tf_op jit(solution)/shard_map/ppermute | solution.py:119
  92.1 0.7 copy-start.1
  92.8 9.0 %collective-permute-start.5 = (bf16[64,2048]{1,0:T(8,128)(2,1)S(1)}, bf16[64,2048]{1,0:T(8,128)(2,1)}, u32[]{:S(2)}, u32[]{:S(2)}) collective-permute-start(bf16[64,2048]{1,0:T(8,128)(2,1)S(1)} %collective-permute-done.4.refs_5_), channel_id=1, source_target_pairs={{0,224},{32,0},{64,32},{96,64},{128,96},{160,128},{192,160},{224,1... | collective-permute-start | bytes 786440 | tf_op jit(solution)/shard_map/ppermute | solution.py:120
  101.8 1.0 copy-start.2

commit v3 on v2

--- a/solution.py
+++ b/solution.py
@@ -16,21 +16,16 @@
     return [(y, (y + step) % 8) for y in range(8)]
 
 
-def y_hop(steps):
-    return [(y * 2 + c, (y + steps * (1 - 2 * c)) % 8 * 2 + c) for y in range(8) for c in range(2)]
-
-
 def wide_index(place, core):
     return place % 2 * 4 + core * 2 + place // 2
 
 
-def x_hop(first):
-    pairs = []
-    for place in range(4):
-        for core in range(2):
-            step = 1 if (core == 0) == first else -1
-            pairs.append((wide_index(place, core), wide_index((place + step) % 4, core)))
-    return pairs
+def x_hop():
+    return [
+        (wide_index(place, core), wide_index((place + 1 - 2 * core) % 4, core))
+        for place in range(4)
+        for core in range(2)
+    ]
 
 
 def pack(values):
@@ -55,7 +50,7 @@
         at = lax.rem(y - steps + 8, 8)
         bring(columns[i], left.at[pl.ds(pl.multiple_of(at * 64, 64), 64), :])
     sign = 1 - 2 * core
-    for i, steps in enumerate((0, 1, 2, -1)):
+    for i, steps in enumerate((0, 1, 2, 3)):
         for near in range(2):
             step = sign * steps if near else -sign * steps
             source = lax.rem(place - step + 8, 4)
@@ -118,15 +113,14 @@
     down2 = lax.ppermute(own, "y", ring(-2))
     up3 = lax.ppermute(up2, "y", ring(1))
     down3 = lax.ppermute(down2, "y", ring(-1))
-    far = lax.ppermute(jnp.where(core == 0, up2, down2), ("y", "core"), y_hop(2))
+    far = lax.ppermute(up2, "y", ring(2))
     columns = [own, up1, up2, up3, down1, down2, down3, far]
     virt_rows = unpack(got[:, 16:]).reshape(64, 32, 64)
     occupied = jnp.einsum("pms,ml->pls", virt_rows, occ_density, preferred_element_type=jnp.float32)
     occupied = lax.optimization_barrier(occupied.astype(jnp.bfloat16).reshape(64, 2048))
-    near = lax.ppermute(occupied, WIDE, x_hop(True))
-    back = lax.ppermute(occupied, WIDE, x_hop(False))
-    far = lax.ppermute(near, WIDE, x_hop(True))
-    mine = [occupied, near, far, back]
+    mine = [occupied]
+    for _ in range(3):
+        mine.append(lax.ppermute(mine[-1], WIDE, x_hop()))
     other = lax.ppermute(jnp.stack(mine), "core", [(0, 1), (1, 0)])
     place = lax.axis_index("x_hi") * 2 + lax.axis_index("x_lo")
     where = jnp.stack([lax.axis_index("y"), place, core]).astype(jnp.int32)

time: 132 us -> 139 us (1.053)
  the two profiles are of different devices: /device:TPU:6 before, /device:TPU:14 now
where the time goes in v3:
time: 139 us; the launch traced here: 138 us
  blocking collectives  58.2 us (42%)
  starting transfers between devices  38.5 us (28%)
  waiting for transfers between devices  28.5 us (21%)
  local copies, waits for them, and re-layouts  7.06 us (5%)
  Pallas kernels  3.25 us (2%)
  other arithmetic  1.87 us (1%)
    all_to_all x1, blocking collectives, body(): got = lax.all_to_all(both, PLANE, 0, 0, tiled=True)  32.2 us
    all_to_all x1, blocking collectives, body(): got = lax.all_to_all(tiles, PLANE, 0, 0, tiled=True)  26 us
    ppermute x3, waiting for transfers between devices, body(): mine.append(lax.ppermute(mine[-1], WIDE, x_hop()))  14.7 us
    ppermute x3, starting transfers between devices, body(): mine.append(lax.ppermute(mine[-1], WIDE, x_hop()))  10.3 us
    ppermute x1, waiting for transfers between devices, body(): far = lax.ppermute(up2, 'y', ring(2))  8.89 us
    ppermute x1, starting transfers between devices, body(): far = lax.ppermute(up2, 'y', ring(2))  6.5 us
    ppermute x1, waiting for transfers between devices, body(): up2 = lax.ppermute(own, 'y', ring(2))  4.9 us
    ppermute x1, starting transfers between devices, body(): up2 = lax.ppermute(own, 'y', ring(2))  4.5 us
  transfers between devices with their start and end apart: 11, of which 5 were waited for; matrix products, arithmetic and copies ran while one was open for 0% of the time, Pallas kernels for 0%

profile of v3, /device:TPU:14, one launch (start us, length us, event | category | flops | bytes accessed | tf_op | source)
XLA Modules:
  0.0 138.3 jit_solution(6235728519527962436)
XLA Ops:
  0.0 1.1 reshape.51
  1.1 0.0 copy-start.5
  1.2 0.3 reshape.49
  1.5 0.3 copy-done.5
  1.8 0.1 broadcast_in_dim.23
  2.0 0.3 convolution_convert_fusion.1
  2.4 0.3 reshape_reshape.8
  2.6 0.5 copy.25
  3.2 0.2 reshape.52
  3.4 0.6 fusion.1
  4.0 0.2 reshape.50
  4.3 32.2 %all_to_all.10 = bf16[64,32,128]{2,1,0:T(8,128)(2,1)S(1)} all-to-all(bf16[64,32,128]{2,1,0:T(8,128)(2,1)S(1)} %pad_maximum_fusion.1), channel_id=1, replica_groups=mesh['x_lo'=2,'y'=8,'core'=2,'z'=8,'x_hi'=2] {'x_lo','core','z','x_hi'}, dimensions={0} | all-to-all | bytes 1048576 | tf_op jit(solution)/shard_map/all_to_all | solution.py:107
  36.5 0.1 copy.15
  36.6 0.0 copy-start.4
  36.6 0.2 reshape_reshape.9
  36.9 0.4 copy-done.4
  37.3 0.3 fusion
  37.6 0.5 reshape.56
  38.1 2.2 %collective-permute-start.7 = (bf16[64,2048]{1,0:T(8,128)(2,1)S(1)}, bf16[64,2048]{1,0:T(8,128)(2,1)S(1)}, u32[]{:S(2)}, u32[]{:S(2)}) collective-permute-start(bf16[64,2048]{1,0:T(8,128)(2,1)S(1)} %reshape.56), channel_id=1, source_target_pairs={{0,256},{16,273},{256,1},{272,16},{1,257},{17,272},{257,0},{273,17... | collective-permute-start | bytes 786440 | tf_op jit(solution)/shard_map/ppermute | solution.py:123
  40.3 6.0 %collective-permute-done.7 = bf16[64,2048]{1,0:T(8,128)(2,1)S(1)} collective-permute-done((bf16[64,2048]{1,0:T(8,128)(2,1)S(1)}, bf16[64,2048]{1,0:T(8,128)(2,1)S(1)}, u32[]{:S(2)}, u32[]{:S(2)}) %collective-permute-start.7) | collective-permute-done | bytes 262176 | tf_op jit(solution)/shard_map/ppermute | solution.py:123
  46.3 3.4 %collective-permute-start.8 = (bf16[64,2048]{1,0:T(8,128)(2,1)S(1)}, bf16[64,2048]{1,0:T(8,128)(2,1)S(1)}, u32[]{:S(2)}, u32[]{:S(2)}) collective-permute-start(bf16[64,2048]{1,0:T(8,128)(2,1)S(1)} %collective-permute-done.7), channel_id=1, source_target_pairs={{0,256},{16,273},{256,1},{272,16},{1,257},{17,272},{257,0},{273,17... | collective-permute-start | bytes 786440 | tf_op jit(solution)/shard_map/ppermute | solution.py:123
  49.8 4.8 %collective-permute-done.8 = bf16[64,2048]{1,0:T(8,128)(2,1)S(1)} collective-permute-done((bf16[64,2048]{1,0:T(8,128)(2,1)S(1)}, bf16[64,2048]{1,0:T(8,128)(2,1)S(1)}, u32[]{:S(2)}, u32[]{:S(2)}) %collective-permute-start.8) | collective-permute-done | bytes 262176 | tf_op jit(solution)/shard_map/ppermute | solution.py:123
  54.6 4.7 %collective-permute-start.9 = (bf16[64,2048]{1,0:T(8,128)(2,1)S(1)}, bf16[64,2048]{1,0:T(8,128)(2,1)S(1)}, u32[]{:S(2)}, u32[]{:S(2)}) collective-permute-start(bf16[64,2048]{1,0:T(8,128)(2,1)S(1)} %collective-permute-done.8), channel_id=1, source_target_pairs={{0,256},{16,273},{256,1},{272,16},{1,257},{17,272},{257,0},{273,17... | collective-permute-start | bytes 786440 | tf_op jit(solution)/shard_map/ppermute | solution.py:123
  59.3 3.9 %collective-permute-done.9 = bf16[64,2048]{1,0:T(8,128)(2,1)S(1)} collective-permute-done((bf16[64,2048]{1,0:T(8,128)(2,1)S(1)}, bf16[64,2048]{1,0:T(8,128)(2,1)S(1)}, u32[]{:S(2)}, u32[]{:S(2)}) %collective-permute-start.9) | collective-permute-done | bytes 262176 | tf_op jit(solution)/shard_map/ppermute | solution.py:123
  63.1 1.1 pad_maximum_fusion
  64.2 1.9 %collective-permute-start.10 = (bf16[4,64,2048]{2,1,0:T(8,128)(2,1)}, bf16[4,64,2048]{2,1,0:T(8,128)(2,1)S(1)}, u32[]{:S(2)}, u32[]{:S(2)}) collective-permute-start(bf16[4,64,2048]{2,1,0:T(8,128)(2,1)} %pad_maximum_fusion), channel_id=1, source_target_pairs={{0,16},{16,0},{1,17},{17,1},{2,18},{18,2},{3,19},{19,3},{4,20},{20... | collective-permute-start | bytes 3145736 | tf_op jit(solution)/shard_map/ppermute | solution.py:124
  66.2 0.1 copy.14
  66.2 0.1 copy.26
  66.3 4.5 %collective-permute-start.1 = (bf16[64,2048]{1,0:T(8,128)(2,1)S(1)}, bf16[64,2048]{1,0:T(8,128)(2,1)S(1)}, u32[]{:S(2)}, u32[]{:S(2)}) collective-permute-start(bf16[64,2048]{1,0:T(8,128)(2,1)S(1)} %bitcast.44), channel_id=1, source_target_pairs={{0,64},{32,96},{64,128},{96,160},{128,192},{160,224},{192,0},{224,... | collective-permute-start | bytes 786440 | tf_op jit(solution)/shard_map/ppermute | solution.py:112
  70.8 3.5 %collective-permute-start.4 = (bf16[64,2048]{1,0:T(8,128)(2,1)S(1)}, bf16[64,2048]{1,0:T(8,128)(2,1)S(1)}, u32[]{:S(2)}, u32[]{:S(2)}) collective-permute-start(bf16[64,2048]{1,0:T(8,128)(2,1)S(1)} %bitcast.45), channel_id=1, source_target_pairs={{0,192},{32,224},{64,0},{96,32},{128,64},{160,96},{192,128},{224,1... | collective-permute-start | bytes 786440 | tf_op jit(solution)/shard_map/ppermute | solution.py:113
  74.3 3.2 %collective-permute-start = (bf16[64,2048]{1,0:T(8,128)(2,1)S(1)}, bf16[64,2048]{1,0:T(8,128)(2,1)S(1)}, u32[]{:S(2)}, u32[]{:S(2)}) collective-permute-start(bf16[64,2048]{1,0:T(8,128)(2,1)S(1)} %bitcast.46), channel_id=1, source_target_pairs={{0,32},{32,64},{64,96},{96,128},{128,160},{160,192},{192,224},{224... | collective-permute-start | bytes 786440 | tf_op jit(solution)/shard_map/ppermute | solution.py:110
  77.4 2.7 %collective-permute-start.3 = (bf16[64,2048]{1,0:T(8,128)(2,1)S(1)}, bf16[64,2048]{1,0:T(8,128)(2,1)}, u32[]{:S(2)}, u32[]{:S(2)}) collective-permute-start(bf16[64,2048]{1,0:T(8,128)(2,1)S(1)} %bitcast.47), channel_id=1, source_target_pairs={{0,224},{32,0},{64,32},{96,64},{128,96},{160,128},{192,160},{224,1... | collective-permute-start | bytes 786440 | tf_op jit(solution)/shard_map/ppermute | solution.py:111
  80.1 4.9 %collective-permute-done.1.refs_2_ = bf16[64,2048]{1,0:T(8,128)(2,1)S(1)} collective-permute-done((bf16[64,2048]{1,0:T(8,128)(2,1)S(1)}, bf16[64,2048]{1,0:T(8,128)(2,1)S(1)}, u32[]{:S(2)}, u32[]{:S(2)}) %collective-permute-start.1) | collective-permute-done | bytes 262176 | tf_op jit(solution)/shard_map/ppermute | solution.py:112
  85.0 2.4 %collective-permute-start.2 = (bf16[64,2048]{1,0:T(8,128)(2,1)S(1)}, bf16[64,2048]{1,0:T(8,128)(2,1)}, u32[]{:S(2)}, u32[]{:S(2)}) collective-permute-start(bf16[64,2048]{1,0:T(8,128)(2,1)S(1)} %collective-permute-done.1.refs_2_), channel_id=1, source_target_pairs={{0,32},{32,64},{64,96},{96,128},{128,160},{160,192},{192,224},{224... | collective-permute-start | bytes 786440 | tf_op jit(solution)/shard_map/ppermute | solution.py:114
  87.5 0.0 collective-permute-done.4.refs_5_
  87.5 6.5 %collective-permute-start.6 = (bf16[64,2048]{1,0:T(8,128)(2,1)S(1)}, bf16[64,2048]{1,0:T(8,128)(2,1)}, u32[]{:S(2)}, u32[]{:S(2)}) collective-permute-start(bf16[64,2048]{1,0:T(8,128)(2,1)S(1)} %collective-permute-done.1.refs_2_), channel_id=1, source_target_pairs={{0,64},{32,96},{64,128},{96,160},{128,192},{160,224},{192,0},{224,... | collective-permute-start | bytes 786440 | tf_op jit(solution)/shard_map/ppermute | solution.py:116
  94.0 0.0 collective-permute-done.refs_1_
  94.0 0.7 copy-done.1
  94.7 3.6 %collective-permute-start.5 = (bf16[64,2048]{1,0:T(8,128)(2,1)S(1)}, bf16[64,2048]{1,0:T(8,128)(2,1)}, u32[]{:S(2)}, u32[]{:S(2)}) collective-permute-start(bf16[64,2048]{1,0:T(8,128)(2,1)S(1)} %collective-permute-done.4.refs_5_), channel_id=1, source_target_pairs={{0,224},{32,0},{64,32},{96,64},{128,96},{160,128},{192,160},{224,1... | collective-permute-start | bytes 786440 | tf_op jit(solution)/shard_map/ppermute | solution.py:115
  98.3 0.1 pad_add_fusion.where_ref
  98.3 0.0 collective-permute-done.3.refs_4_
  98.3 0.0 collective-permute-done.2.refs_3_
  98.3 8.9 %collective-permute-done.6.refs_7_ = bf16[64,2048]{1,0:T(8,128)(2,1)} collective-permute-done((bf16[64,2048]{1,0:T(8,128)(2,1)S(1)}, bf16[64,2048]{1,0:T(8,128)(2,1)}, u32[]{:S(2)}, u32[]{:S(2)}) %collective-permute-start.6) | collective-permute-done | bytes 262176 | tf_op jit(solution)/shard_map/ppermute | solution.py:116
  107.2 0.9 copy-done.2
  108.2 3.2 %shard_map.46 = bf16[64,32,128]{2,1,0:T(8,128)(2,1)S(1)} custom-call(s32[3]{0:T(128)S(1)} %pad_add_fusion.where_ref, bf16[64,2048]{1,0:T(8,128)(2,1)S(1)} %bitcast.48, bf16[64,2048]{1,0:T(8,128)(2,1)S(1)} %copy-done.2, bf16[64,2048]{1,0:T(8,128)(2,1)S(1)} %collective-permute-done.1.refs_2_, bf16[64,2048]{1,0:T(8,128)(2,1)} %collective-permute-done.2.refs_3_, ...), custom_call_target="tpu_custom_call" | custom-call | flops 1073741824 | bytes 4194304 | tf_op jit(solution)/shard_map/pallas_call | solution.py:79
  111.4 26.0 %all_to_all.11 = bf16[64,32,128]{2,1,0:T(8,128)(2,1)S(1)} all-to-all(bf16[64,32,128]{2,1,0:T(8,128)(2,1)S(1)} %shard_map.46), channel_id=1, replica_groups=mesh['x_lo'=2,'y'=8,'core'=2,'z'=8,'x_hi'=2] {'x_lo','core','z','x_hi'}, dimensions={0} | all-to-all | bytes 1048576 | tf_op jit(solution)/shard_map/all_to_all | solution.py:128
  137.4 0.1 convert_reduce_fusion
  137.5 0.8 copy.18
  (13 shorter events, 0.1 us)
Async XLA Ops:
  0.0 2.0 %copy-start = (bf16[512,512]{1,0:T(8,128)(2,1)S(1)}, bf16[512,512]{1,0:T(8,128)(2,1)}, u32[]{:S(2)}) copy-start(bf16[512,512]{1,0:T(8,128)(2,1)} %param.6) | copy-start | bytes 1572868
  0.0 1.1 copy-start.3
  1.1 0.7 copy-start.5
  36.6 0.7 copy-start.4
  38.1 8.3 %collective-permute-start.7 = (bf16[64,2048]{1,0:T(8,128)(2,1)S(1)}, bf16[64,2048]{1,0:T(8,128)(2,1)S(1)}, u32[]{:S(2)}, u32[]{:S(2)}) collective-permute-start(bf16[64,2048]{1,0:T(8,128)(2,1)S(1)} %reshape.56), channel_id=1, source_target_pairs={{0,256},{16,273},{256,1},{272,16},{1,257},{17,272},{257,0},{273,17... | collective-permute-start | bytes 786440 | tf_op jit(solution)/shard_map/ppermute | solution.py:123
  46.3 8.3 %collective-permute-start.8 = (bf16[64,2048]{1,0:T(8,128)(2,1)S(1)}, bf16[64,2048]{1,0:T(8,128)(2,1)S(1)}, u32[]{:S(2)}, u32[]{:S(2)}) collective-permute-start(bf16[64,2048]{1,0:T(8,128)(2,1)S(1)} %collective-permute-done.7), channel_id=1, source_target_pairs={{0,256},{16,273},{256,1},{272,16},{1,257},{17,272},{257,0},{273,17... | collective-permute-start | bytes 786440 | tf_op jit(solution)/shard_map/ppermute | solution.py:123
  54.6 8.5 %collective-permute-start.9 = (bf16[64,2048]{1,0:T(8,128)(2,1)S(1)}, bf16[64,2048]{1,0:T(8,128)(2,1)S(1)}, u32[]{:S(2)}, u32[]{:S(2)}) collective-permute-start(bf16[64,2048]{1,0:T(8,128)(2,1)S(1)} %collective-permute-done.8), channel_id=1, source_target_pairs={{0,256},{16,273},{256,1},{272,16},{1,257},{17,272},{257,0},{273,17... | collective-permute-start | bytes 786440 | tf_op jit(solution)/shard_map/ppermute | solution.py:123
  64.2 43.0 %collective-permute-start.10 = (bf16[4,64,2048]{2,1,0:T(8,128)(2,1)}, bf16[4,64,2048]{2,1,0:T(8,128)(2,1)S(1)}, u32[]{:S(2)}, u32[]{:S(2)}) collective-permute-start(bf16[4,64,2048]{2,1,0:T(8,128)(2,1)} %pad_maximum_fusion), channel_id=1, source_target_pairs={{0,16},{16,0},{1,17},{17,1},{2,18},{18,2},{3,19},{19,3},{4,20},{20... | collective-permute-start | bytes 3145736 | tf_op jit(solution)/shard_map/ppermute | solution.py:124
  66.3 18.7 %collective-permute-start.1 = (bf16[64,2048]{1,0:T(8,128)(2,1)S(1)}, bf16[64,2048]{1,0:T(8,128)(2,1)S(1)}, u32[]{:S(2)}, u32[]{:S(2)}) collective-permute-start(bf16[64,2048]{1,0:T(8,128)(2,1)S(1)} %bitcast.44), channel_id=1, source_target_pairs={{0,64},{32,96},{64,128},{96,160},{128,192},{160,224},{192,0},{224,... | collective-permute-start | bytes 786440 | tf_op jit(solution)/shard_map/ppermute | solution.py:112
  70.8 16.6 %collective-permute-start.4 = (bf16[64,2048]{1,0:T(8,128)(2,1)S(1)}, bf16[64,2048]{1,0:T(8,128)(2,1)S(1)}, u32[]{:S(2)}, u32[]{:S(2)}) collective-permute-start(bf16[64,2048]{1,0:T(8,128)(2,1)S(1)} %bitcast.45), channel_id=1, source_target_pairs={{0,192},{32,224},{64,0},{96,32},{128,64},{160,96},{192,128},{224,1... | collective-permute-start | bytes 786440 | tf_op jit(solution)/shard_map/ppermute | solution.py:113
  74.3 19.7 %collective-permute-start = (bf16[64,2048]{1,0:T(8,128)(2,1)S(1)}, bf16[64,2048]{1,0:T(8,128)(2,1)S(1)}, u32[]{:S(2)}, u32[]{:S(2)}) collective-permute-start(bf16[64,2048]{1,0:T(8,128)(2,1)S(1)} %bitcast.46), channel_id=1, source_target_pairs={{0,32},{32,64},{64,96},{96,128},{128,160},{160,192},{192,224},{224... | collective-permute-start | bytes 786440 | tf_op jit(solution)/shard_map/ppermute | solution.py:110
  77.4 20.9 %collective-permute-start.3 = (bf16[64,2048]{1,0:T(8,128)(2,1)S(1)}, bf16[64,2048]{1,0:T(8,128)(2,1)}, u32[]{:S(2)}, u32[]{:S(2)}) collective-permute-start(bf16[64,2048]{1,0:T(8,128)(2,1)S(1)} %bitcast.47), channel_id=1, source_target_pairs={{0,224},{32,0},{64,32},{96,64},{128,96},{160,128},{192,160},{224,1... | collective-permute-start | bytes 786440 | tf_op jit(solution)/shard_map/ppermute | solution.py:111
  85.0 13.3 %collective-permute-start.2 = (bf16[64,2048]{1,0:T(8,128)(2,1)S(1)}, bf16[64,2048]{1,0:T(8,128)(2,1)}, u32[]{:S(2)}, u32[]{:S(2)}) collective-permute-start(bf16[64,2048]{1,0:T(8,128)(2,1)S(1)} %collective-permute-done.1.refs_2_), channel_id=1, source_target_pairs={{0,32},{32,64},{64,96},{96,128},{128,160},{160,192},{192,224},{224... | collective-permute-start | bytes 786440 | tf_op jit(solution)/shard_map/ppermute | solution.py:114
  87.5 19.8 %collective-permute-start.6 = (bf16[64,2048]{1,0:T(8,128)(2,1)S(1)}, bf16[64,2048]{1,0:T(8,128)(2,1)}, u32[]{:S(2)}, u32[]{:S(2)}) collective-permute-start(bf16[64,2048]{1,0:T(8,128)(2,1)S(1)} %collective-permute-done.1.refs_2_), channel_id=1, source_target_pairs={{0,64},{32,96},{64,128},{96,160},{128,192},{160,224},{192,0},{224,... | collective-permute-start | bytes 786440 | tf_op jit(solution)/shard_map/ppermute | solution.py:116
  94.0 0.7 copy-start.1
  94.7 12.5 %collective-permute-start.5 = (bf16[64,2048]{1,0:T(8,128)(2,1)S(1)}, bf16[64,2048]{1,0:T(8,128)(2,1)}, u32[]{:S(2)}, u32[]{:S(2)}) collective-permute-start(bf16[64,2048]{1,0:T(8,128)(2,1)S(1)} %collective-permute-done.4.refs_5_), channel_id=1, source_target_pairs={{0,224},{32,0},{64,32},{96,64},{128,96},{160,128},{192,160},{224,1... | collective-permute-start | bytes 786440 | tf_op jit(solution)/shard_map/ppermute | solution.py:115
  107.2 1.0 copy-start.2
